TPU v7x, 32 devices: a whole 2x2x4 slice. The times are simulated.
32 devices in a mesh: tile: 16 (over z, y, x), mode: 2 (over core).
Axes of the slice: x: 2, y: 2, z: 4, core: 2. Of those that a mesh axis runs over, the one named last changes fastest.
Arguments:
- object_tiles: float32 [2, 2048, 2048], P(None, 'tile'), may hold values from -6 to 6
- probe_modes: float32 [4, 2, 256, 256], P('mode'), may hold values from -5 to 5
- amplitudes: float32 [16, 256, 256], P('tile'), may hold values from 0.25 to 4
- scan_offsets: int32 [8192, 2], replicated, may hold values from 0 to 1792, as said below
- slot_scan: int32 [16], P('tile'), may hold values from 0 to 8191, as said below
- slot_count: int32 [16], P('tile'), may hold values from 0 to 1, as said below
Outputs:
- updated_object: float32 [2, 2048, 2048], P(None, 'tile')
- object_gradient: float32 [2, 2048, 2048], P(None, 'tile')
Inputs may be any that keep to these rules, and one draw needn't show every extreme that they name: `scan_offsets`: every patch of 256 x 256 pixels at an offset lies inside the object. `slot_scan`: on every index d of tile but the last, the row offset of each slot's scan position lies in [d * 128, (d + 1) * 128). The positions of one device's slots are distinct. `slot_count`: the live slots of a device are its first ones. The last index of tile holds none, every other holds at least one; some index holds 1.
All inputs are finite; a program needn't handle non-finite values.
Results may differ from a plain program's by a relative error of at most 0.0001.
Values sent between devices are 32-bit elements; how exact they have to be, the bound alone decides.
No kernel may reach another device: no remote copies, remote signals or barrier semaphores. Data moves between devices by JAX's collectives and lax.ppermute only.
A program may use at most 64 MiB of HBM per device.

v0:
```python
import math

import jax
import jax.numpy as jnp
import numpy as np
from jax import lax
from jax.experimental import pallas as pl
from jax.experimental.pallas import tpu as pltpu
from jax.sharding import PartitionSpec as P


FLOOR = 0.25
ALPHA = 0.5
LANES = 128
AXES = ("tile", "mode")
VMEM = pltpu.VMEM
SMEM = pltpu.SMEM


def split(value):
    high = value.astype(jnp.bfloat16)
    low = (value - high.astype(jnp.float32)).astype(jnp.bfloat16)
    return high, low


def matrices(frame):
    half = frame // 2
    pixel = np.arange(half)[:, None]
    wave = np.arange(half)[None, :]
    blocks = []
    for parity in (0, 1):
        phase = 2.0 * math.pi * (pixel * (2 * wave + parity) % frame) / frame
        cos, sin = np.cos(phase) / math.sqrt(frame), np.sin(phase) / math.sqrt(frame)
        forward = np.block([[cos, -sin], [sin, cos]])
        for table in (forward, forward.T):
            high = table.astype(jnp.bfloat16)
            blocks.append(high)
            blocks.append((table - high.astype(np.float64)).astype(jnp.bfloat16))
    return np.stack(blocks)


def lookup(table_ref, scan):
    base = pl.multiple_of((scan // LANES) * LANES, LANES)
    chunk = table_ref[:, pl.ds(base, LANES)].astype(jnp.float32)
    lane = lax.broadcasted_iota(jnp.int32, chunk.shape, 1)
    picked = jnp.where(lane == scan - base, chunk, 0.0)
    row = jnp.sum(picked[0:1]).astype(jnp.int32)
    col = jnp.sum(picked[1:2]).astype(jnp.int32)
    return row, col


def strip_window(object_ref, col):
    blocks = object_ref.shape[2] // LANES
    block, shift = col // LANES, col % LANES
    first = object_ref[:, :, pl.ds(pl.multiple_of(block * LANES, LANES), LANES)]
    second = object_ref[:, :, pl.ds(pl.multiple_of((block + 1) * LANES, LANES), LANES)]
    last = jnp.minimum(block + 2, blocks - 1)
    third = object_ref[:, :, pl.ds(pl.multiple_of(last * LANES, LANES), LANES)]
    lane = lax.broadcasted_iota(jnp.int32, first.shape, 2)
    return jnp.where(lane < shift, third, first), second


def fetch(pairs, sems, first=0):
    copies = [pltpu.make_async_copy(a, b, sems.at[first + index]) for index, (a, b) in enumerate(pairs)]
    for copy in copies:
        copy.start()
    return copies


def select_kernel(own_scan_ref, scan_ref, table_ref, object_ref, out_ref, found_ref):
    odd = lax.axis_index("tile") % 2 == 1
    got, own = lookup(table_ref, scan_ref[0]), lookup(table_ref, own_scan_ref[0])
    low, high = strip_window(object_ref, jnp.where(odd & (lax.axis_index("mode") == 1), own[1], got[1]))
    out_ref[:, :, :LANES] = low
    out_ref[:, :, LANES:] = high
    keep_scalars(found_ref, (*got, *own))


def slots(found_ref, swapped_ref):
    first = lax.axis_index("mode") == 0
    odd = lax.axis_index("tile") % 2 == 1

    def choose(flag, one, two):
        return tuple(jnp.where(flag, a, b) for a, b in zip(one, two))

    got = scalar_of(found_ref, 0), scalar_of(found_ref, 1)
    own = scalar_of(found_ref, 2), scalar_of(found_ref, 3)
    other = scalar_of(swapped_ref, 0), scalar_of(swapped_ref, 1)
    above, further = choose(first, got, other), choose(first, other, got)
    return choose(odd, further, own), above, choose(odd, own, further)


def keep_scalars(out_ref, values):
    for index, value in enumerate(values):
        row = jnp.full((1, out_ref.shape[1]), value, jnp.int32)
        out_ref[index : index + 1] = row.astype(jnp.float32)


def scalar_of(ref, index):
    return jnp.max(ref[index : index + 1]).astype(jnp.int32)


def within(place, strip, height):
    return jnp.clip(place[0] - strip * height, 0, height - 1), place[1]


def roll_into(out_ref, value, row, col, tall_ref):
    frame = value.shape[0]
    half = frame // 2
    turned = pltpu.roll(value, col, 1)
    for index in range(frame // LANES):
        at = slice(index * LANES, (index + 1) * LANES)
        tall_ref[index, :half] = turned[half:, at]
        tall_ref[index, half:] = turned[:, at]
        out_ref[:, at] = tall_ref[index, pl.ds(half - row, frame), :]


def reorder_kernel(own_ref, received_ref, swapped_ref, factor_ref, rows_ref):
    frame = own_ref.shape[1]
    odd = lax.axis_index("tile") % 2 == 1
    moved = jnp.where(lax.axis_index("mode") == 0, received_ref[0], swapped_ref[0])
    value = jnp.where(odd, moved, own_ref[0])
    source = lax.broadcasted_iota(jnp.int32, (frame, frame), 0)
    target = lax.broadcasted_iota(jnp.int32, (frame, frame), 1)
    half = frame // 2
    order = jnp.where(target < half, 2 * target, 2 * target - frame + 1)
    pick = jnp.where(source == order, 1.0, 0.0).astype(jnp.bfloat16)
    high = value.astype(jnp.bfloat16)
    rest = value - high.astype(jnp.float32)
    middle = rest.astype(jnp.bfloat16)
    low = (rest - middle.astype(jnp.float32)).astype(jnp.bfloat16)
    columns = jnp.dot(high, pick, preferred_element_type=jnp.float32)
    columns = columns + jnp.dot(middle, pick, preferred_element_type=jnp.float32)
    columns = columns + jnp.dot(low, pick, preferred_element_type=jnp.float32)
    for index in range(frame // LANES):
        at = slice(index * LANES, (index + 1) * LANES)
        rows_ref[index] = columns[:, at]
        factor_ref[:half, at] = rows_ref[index, pl.ds(0, half, stride=2), :]
        factor_ref[half:, at] = rows_ref[index, pl.ds(1, half, stride=2), :]


def probe_parts(own_probe_ref, other_probe_ref):
    modes = own_probe_ref.shape[0]
    return [ref.at[mode, part] for ref in (own_probe_ref, other_probe_ref) for mode in range(modes) for part in range(2)]


def fill_kernel(own_probe_ref, other_probe_ref, gradient_ref, total_ref, zero_ref, sems):
    zero_ref[...] = jnp.zeros_like(zero_ref)
    step = zero_ref.shape[0]
    copies = []
    for part in range(2):
        for at in range(0, gradient_ref.shape[1], step):
            copies += fetch([(zero_ref, gradient_ref.at[part, at : at + step])], sems, len(copies))
    total = jnp.zeros(total_ref.shape, jnp.float32)
    for source in probe_parts(own_probe_ref, other_probe_ref):
        total = total + source[...] * source[...]
    total_ref[...] = total
    for copy in copies:
        copy.wait()


def prepare_kernel(
    found_ref, swapped_ref, object_ref, own_probe_ref, other_probe_ref, total_ref,
    probe_ref, window_ref, light_ref, place_ref, tall_ref,
):
    sources = probe_parts(own_probe_ref, other_probe_ref)
    height = object_ref.shape[1]
    tile = lax.axis_index("tile")
    odd = tile % 2
    main, _, _ = slots(found_ref, swapped_ref)
    row, col = within(main, tile - 2 * odd, height)
    shift = col % LANES
    for index, source in enumerate(sources):
        roll_into(probe_ref.at[index // 2, index % 2], source[...], row, shift, tall_ref.at[index])
    roll_into(light_ref, total_ref[...], row, shift, tall_ref.at[len(sources)])
    low, high = strip_window(object_ref, col)
    window_ref[:, :, :LANES] = low
    window_ref[:, :, LANES:] = high
    live = jnp.where(odd == 1, (tile >= 2).astype(jnp.int32), 1)
    keep_scalars(place_ref, (jnp.where(odd == 1, 0, row), jnp.where(odd == 1, row, height), live))


def right(value, high, low):
    first, second = split(value)
    return jnp.dot(
        jnp.concatenate([first, second, first], axis=1),
        jnp.concatenate([high, high, low], axis=0),
        preferred_element_type=jnp.float32,
    )


def left(high, low, value):
    first, second = split(value)
    return jnp.dot(
        jnp.concatenate([high, high, low], axis=1),
        jnp.concatenate([first, second, first], axis=0),
        preferred_element_type=jnp.float32,
    )


def transform_rows(probe_ref, start, window_ref, matrix_ref, out_ref):
    modes = probe_ref.shape[0]
    height, frame = window_ref.shape[1:]
    half = frame // 2
    sums, differences = [], []
    for mode in range(modes):
        probe_re = probe_ref[mode, 0, pl.ds(start, height), :]
        probe_im = probe_ref[mode, 1, pl.ds(start, height), :]
        wave_re = probe_re * window_ref[0] - probe_im * window_ref[1]
        wave_im = probe_re * window_ref[1] + probe_im * window_ref[0]
        for pieces, sign in ((sums, 1.0), (differences, -1.0)):
            pieces.append(
                jnp.concatenate(
                    [wave_re[:, :half] + sign * wave_re[:, half:], wave_im[:, :half] + sign * wave_im[:, half:]],
                    axis=1,
                )
            )
    even = right(jnp.concatenate(sums, axis=0), matrix_ref[0], matrix_ref[1])
    odd = right(jnp.concatenate(differences, axis=0), matrix_ref[4], matrix_ref[5])
    for mode in range(modes):
        at = slice(mode * height, (mode + 1) * height)
        out_ref[mode, 0] = jnp.concatenate([even[at, :half], odd[at, :half]], axis=1)
        out_ref[mode, 1] = jnp.concatenate([even[at, half:], odd[at, half:]], axis=1)


def strip_kernel(own_ref, received_ref, probe_ref, matrix_ref, own_out_ref, out_ref):
    height = received_ref.shape[1]
    start = pl.multiple_of((1 - lax.axis_index("mode")) * height, height)
    transform_rows(probe_ref, 0, own_ref, matrix_ref, own_out_ref)
    transform_rows(probe_ref, start, received_ref, matrix_ref, out_ref)


def wave_kernel(
    place_ref, window_ref, received_ref, swapped_ref, own_ref, first_ref, probe_ref, amplitude_ref, light_ref,
    matrix_ref, send_ref, keep_ref, patch_ref, far_ref, second_ref,
):
    modes, _, frame, _ = probe_ref.shape
    height = window_ref.shape[1]
    half = frame // 2
    core = lax.axis_index("mode")
    low, high = place_ref[0:1, :1].astype(jnp.int32), place_ref[1:2, :1].astype(jnp.int32)
    transform_rows(probe_ref, pl.multiple_of(core * height, height), swapped_ref, matrix_ref, second_ref)
    level = lax.broadcasted_iota(jnp.int32, (height, frame), 0)

    def assemble(own, got, given):
        nearer = jnp.where(core == 0, got, given)
        farther = jnp.where(core == 0, given, got)
        return jnp.where((level >= low) & (level < high), own, farther), nearer

    for part in range(2):
        top, bottom = assemble(window_ref[part], received_ref[part], swapped_ref[part])
        patch_ref[part, :height] = top
        patch_ref[part, height:] = bottom
    intensity = jnp.zeros((frame, frame), jnp.float32)
    for mode in range(modes):
        top_re, bottom_re = assemble(own_ref[mode, 0], first_ref[mode, 0], second_ref[mode, 0])
        top_im, bottom_im = assemble(own_ref[mode, 1], first_ref[mode, 1], second_ref[mode, 1])
        added = jnp.concatenate([top_re + bottom_re, top_im + bottom_im], axis=0)
        taken = jnp.concatenate([top_re - bottom_re, top_im - bottom_im], axis=0)
        even = left(matrix_ref[2], matrix_ref[3], added)
        odd = left(matrix_ref[6], matrix_ref[7], taken)
        far_ref[mode, 0] = even
        far_ref[mode, 1] = odd
        squares = jnp.concatenate(
            [even[:half] * even[:half] + even[half:] * even[half:], odd[:half] * odd[:half] + odd[half:] * odd[half:]],
            axis=0,
        )
        intensity = intensity + squares
    factor = amplitude_ref[...] * lax.rsqrt(jnp.maximum(intensity, FLOOR))
    grad_re = jnp.zeros((frame, frame), jnp.float32)
    grad_im = jnp.zeros((frame, frame), jnp.float32)
    even_factor = jnp.concatenate([factor[:half], factor[:half]], axis=0)
    odd_factor = jnp.concatenate([factor[half:], factor[half:]], axis=0)
    evens, odds = [], []
    for mode in range(modes):
        even = left(matrix_ref[0], matrix_ref[1], far_ref[mode, 0] * even_factor)
        odd = left(matrix_ref[4], matrix_ref[5], far_ref[mode, 1] * odd_factor)
        top, bottom = even + odd, even - odd
        mid_re = jnp.concatenate([top[:half], bottom[:half]], axis=0)
        mid_im = jnp.concatenate([top[half:], bottom[half:]], axis=0)
        evens.append(jnp.concatenate([mid_re[:, :half], mid_im[:, :half]], axis=1))
        odds.append(jnp.concatenate([mid_re[:, half:], mid_im[:, half:]], axis=1))
    even = right(jnp.concatenate(evens, axis=0), matrix_ref[2], matrix_ref[3])
    odd = right(jnp.concatenate(odds, axis=0), matrix_ref[6], matrix_ref[7])
    fores, afts = even + odd, even - odd
    for mode in range(modes):
        fore = fores[mode * frame : (mode + 1) * frame]
        aft = afts[mode * frame : (mode + 1) * frame]
        back_re = jnp.concatenate([fore[:, :half], aft[:, :half]], axis=1)
        back_im = jnp.concatenate([fore[:, half:], aft[:, half:]], axis=1)
        probe_re, probe_im = probe_ref[mode, 0], probe_ref[mode, 1]
        grad_re = grad_re + (probe_re * back_re + probe_im * back_im)
        grad_im = grad_im + (probe_re * back_im - probe_im * back_re)
    live = place_ref[2:3, :1]
    grad_re = (grad_re - light_ref[...] * patch_ref[0]) * live
    grad_im = (grad_im - light_ref[...] * patch_ref[1]) * live
    send_ref[:height] = jnp.where(core == 0, grad_re[height:], grad_re[:height])
    send_ref[height : 2 * height] = jnp.where(core == 0, grad_im[height:], grad_im[:height])
    send_ref[2 * height :] = jnp.broadcast_to(live, (8, frame))
    keep_ref[0] = grad_re[:height]
    keep_ref[1] = grad_im[:height]


def covers(col, block, low, high, lane):
    start, shift = col // LANES, col % LANES
    distance = block - start
    value = jnp.where(distance == 1, high, low)
    first = jnp.where(distance == 0, shift, jnp.where(distance == 1, 0, LANES))
    last = jnp.where(distance == 2, shift, 0)
    keep = (lane >= first) | (lane < last)
    return jnp.where(keep, value, 0.0)


def base_kernel(
    place_ref, found_ref, swapped_ref, object_ref, keep_ref, light_ref, plain_ref,
    old_gradient_ref,
    updated_ref, gradient_ref, total_ref, weight_ref, first_ref, second_ref, others_ref, new_ref, tall_ref, turned_ref, sems, fills,
):
    del old_gradient_ref
    height, breadth = object_ref.shape[1:]
    tile = lax.axis_index("tile")
    core = lax.axis_index("mode")
    fill = pltpu.make_async_copy(object_ref, updated_ref, fills.at[0])
    fill.start()
    total_ref[...] = jnp.zeros_like(total_ref)
    weight_ref[...] = jnp.zeros_like(weight_ref)
    odd = tile % 2
    (_, col), above, third = slots(found_ref, swapped_ref)
    live = place_ref[2:3, :1]
    start, stop = place_ref[0:1, :1].astype(jnp.int32), place_ref[1:2, :1].astype(jnp.int32)
    lane = lax.broadcasted_iota(jnp.int32, (height, LANES), 1)
    level = lax.broadcasted_iota(jnp.int32, (height, LANES), 0)
    kept = (level >= start) & (level < stop)
    for slot in range(3):
        block = jnp.minimum(col // LANES + slot, breadth // LANES - 1)
        at = pl.ds(pl.multiple_of(block * LANES, LANES), LANES)
        light = covers(col, block, light_ref[:height, :LANES], light_ref[:height, LANES:], lane)
        weight = jnp.where(kept, light * live, 0.0)
        weight_ref[:, at] = weight
        scale = 1.0 / (weight + ALPHA)
        for part in range(2):
            change = covers(col, block, keep_ref[part, :, :LANES], keep_ref[part, :, LANES:], lane)
            change = jnp.where(kept, change, 0.0)
            total_ref[part, :, at] = change
            new_ref[slot, part] = object_ref[part, :, at] + change * scale
    places = []
    for place, strip, far in ((above, tile - 1, False), (third, tile - 2 + 2 * odd, True)):
        row, start = within(place, strip, height)
        index = int(far)
        roll_into(turned_ref.at[index], plain_ref[...], row, start % LANES, tall_ref.at[index])
        turned = turned_ref[index]
        begin = jnp.where(odd == 1, row, 0) if far else 0
        end = jnp.where(odd == 1, height, row) if far else height
        places.append((start, begin, end, turned[:height] if far else turned[height:]))
    chosen = []
    for slot, out_ref in ((0, first_ref), (1, second_ref)):
        direct = core == slot
        near, far = places
        out_ref[...] = jnp.where(direct, near[3], far[3])
        chosen += [jnp.where(direct, near[index], far[index]) for index in range(3)]
    keep_scalars(others_ref, chosen)
    fill.wait()
    copies = []
    for slot in range(3):
        block = jnp.minimum(col // LANES + slot, breadth // LANES - 1)
        at = pl.ds(pl.multiple_of(block * LANES, LANES), LANES)
        copies.append(write(slot, col, block, at, total_ref.at[:, :, at], new_ref, gradient_ref, updated_ref, sems))
    finish(copies)


def write(slot, col, block, at, source, new_ref, gradient_ref, updated_ref, sems):
    fresh = col // LANES + slot == block
    one = pltpu.make_async_copy(source, gradient_ref.at[:, :, at], sems.at[2 * slot])
    two = pltpu.make_async_copy(new_ref.at[slot], updated_ref.at[:, :, at], sems.at[2 * slot + 1])

    @pl.when(fresh)
    def _():
        one.start()
        two.start()

    return fresh, one, two


def finish(copies):
    for fresh, one, two in copies:

        @pl.when(fresh)
        def _(one=one, two=two):
            one.wait()
            two.wait()


def add_windows(windows, main, object_ref, total_ref, weight_ref, updated_ref, gradient_ref, new_ref, sum_ref, sems):
    height, breadth = object_ref.shape[1:]
    lane = lax.broadcasted_iota(jnp.int32, (height, LANES), 1)
    level = lax.broadcasted_iota(jnp.int32, (height, LANES), 0)
    col = windows[main][0]
    copies = []
    for slot in range(3):
        block = jnp.minimum(col // LANES + slot, breadth // LANES - 1)
        at = pl.ds(pl.multiple_of(block * LANES, LANES), LANES)
        weight = weight_ref[:, at]
        sums = [total_ref[0, :, at], total_ref[1, :, at]]
        for start, begin, end, light_ref, change_ref in windows:
            inside = (level >= begin) & (level < end)
            live = change_ref[2 * height : 2 * height + 1, :1]
            light = covers(start, block, light_ref[:, :LANES], light_ref[:, LANES:], lane)
            weight = weight + jnp.where(inside, light, 0.0) * live
            for part in range(2):
                rows = slice(part * height, (part + 1) * height)
                change = covers(start, block, change_ref[rows, :LANES], change_ref[rows, LANES:], lane)
                sums[part] = sums[part] + jnp.where(inside, change, 0.0)
        scale = 1.0 / (weight + ALPHA)
        for part in range(2):
            sum_ref[slot, part] = sums[part]
            new_ref[slot, part] = object_ref[part, :, at] + sums[part] * scale
        copies.append(write(slot, col, block, at, sum_ref.at[slot], new_ref, gradient_ref, updated_ref, sems))
    finish(copies)


def first_kernel(
    others_ref, object_ref, total_ref, weight_ref, first_ref, received_ref, old_updated_ref, old_gradient_ref,
    updated_ref, gradient_ref, new_ref, sum_ref, sems,
):
    del old_updated_ref, old_gradient_ref
    windows = [(*(scalar_of(others_ref, index) for index in range(3)), first_ref, received_ref)]
    add_windows(windows, 0, object_ref, total_ref, weight_ref, updated_ref, gradient_ref, new_ref, sum_ref, sems)


def second_kernel(
    others_ref, object_ref, total_ref, weight_ref, first_ref, second_ref, received_ref, swapped_ref,
    old_updated_ref, old_gradient_ref, updated_ref, gradient_ref, new_ref, sum_ref, sems,
):
    del old_updated_ref, old_gradient_ref
    windows = [
        (*(scalar_of(others_ref, index) for index in range(3)), first_ref, received_ref),
        (*(scalar_of(others_ref, index) for index in range(3, 6)), second_ref, swapped_ref),
    ]
    add_windows(windows, 1, object_ref, total_ref, weight_ref, updated_ref, gradient_ref, new_ref, sum_ref, sems)


def call(kernel, out_shape, in_specs, out_specs, scratch=(), mebibytes=16, aliases=None):
    return pl.pallas_call(
        kernel,
        out_shape=out_shape,
        in_specs=in_specs,
        out_specs=out_specs,
        scratch_shapes=list(scratch),
        input_output_aliases=aliases or {},
        compiler_params=pltpu.CompilerParams(vmem_limit_bytes=mebibytes << 20),
        cost_estimate=pl.CostEstimate(flops=5000000, bytes_accessed=5000000, transcendentals=0),
    )


def space(where):
    return pl.BlockSpec(memory_space=where)


def shape(*dims, dtype=jnp.float32):
    return jax.ShapeDtypeStruct(dims, dtype)


def solution(mesh):
    tiles, cores = mesh.shape["tile"], mesh.shape["mode"]
    up = [(2 * t, 2 * (t + 1)) for t in range(tiles - 1)] + [(2 * t + 1, 2 * (t + 2) + 1) for t in range(tiles - 2)]
    gather = [(2 * t, 2 * (t ^ 1)) for t in range(tiles)]
    gather += [(2 * t + 1, 2 * (t - 2) + 1) for t in range(2, tiles, 2)]
    gather += [(2 * t + 1, 2 * (t + 2) + 1) for t in range(1, tiles - 2, 2)]
    spread = [(target, source) for source, target in gather]
    onward = [(2 * t, 2 * (t + 2)) for t in range(1, tiles - 2, 2)]
    swap = [(2 * t + core, 2 * t + 1 - core) for t in range(tiles) for core in range(2)]
    assert cores == 2 and tiles % 2 == 0

    def move(value, pairs):
        return lax.ppermute(value, AXES, pairs)

    def step(object_tiles, probe_modes, amplitudes, scan_offsets, slot_scan, slot_count):
        height, breadth = object_tiles.shape[1:]
        modes, _, frame, _ = probe_modes.shape
        assert slot_scan.shape[0] == 1 and frame == 2 * height and height == LANES
        table = scan_offsets.T
        matrix = jnp.asarray(matrices(frame))
        received_scan = move(slot_scan, up)
        staged = move(object_tiles, swap)
        table = move(table, swap)
        own_scan = move(slot_scan, swap)
        other_probe = move(probe_modes, swap)
        received_amplitude = move(amplitudes, onward)
        window, found = call(
            select_kernel,
            (shape(2, height, frame), shape(8, LANES)),
            [space(SMEM)] * 2 + [space(VMEM)] * 2,
            [space(VMEM)] * 2,
        )(own_scan, received_scan, table, staged)
        received = move(window, gather)
        swapped_found = move(found, swap)
        swapped_amplitude = move(received_amplitude, swap)
        strip = shape(2 * modes, 2, height, frame)
        whole = shape(2, height, breadth)
        gradient, plain = call(
            fill_kernel,
            (whole, shape(frame, frame)),
            [space(VMEM)] * 2,
            [space(pl.ANY), space(VMEM)],
            [pltpu.VMEM((height // 8, breadth), jnp.float32), pltpu.SemaphoreType.DMA((16,))],
        )(probe_modes, other_probe)
        probe, own_window, light, place = call(
            prepare_kernel,
            (
                shape(2 * modes, 2, frame, frame),
                shape(2, height, frame),
                shape(frame, frame),
                shape(8, LANES),
            ),
            [space(VMEM)] * 6,
            [space(VMEM)] * 4,
            [pltpu.VMEM((4 * modes + 1, frame // LANES, frame + height, LANES), jnp.float32)],
        )(found, swapped_found, staged, probe_modes, other_probe, plain)
        swapped = move(received, swap)
        amplitude = call(
            reorder_kernel,
            shape(frame, frame),
            [space(VMEM)] * 3,
            space(VMEM),
            [pltpu.VMEM((frame // LANES, frame, LANES), jnp.float32)],
        )(amplitudes, received_amplitude, swapped_amplitude)
        own_strip, first_strip = call(strip_kernel, (strip, strip), [space(VMEM)] * 4, [space(VMEM)] * 2)(
            own_window, received, probe, matrix
        )
        send, keep = call(
            wave_kernel,
            (shape(2 * height + 8, frame), shape(2, height, frame)),
            [space(VMEM)] * 10,
            [space(VMEM)] * 2,
            [
                pltpu.VMEM((2, frame, frame), jnp.float32),
                pltpu.VMEM((2 * modes, 2, frame, frame), jnp.float32),
                pltpu.VMEM((2 * modes, 2, height, frame), jnp.float32),
            ],
            mebibytes=24,
        )(place, own_window, received, swapped, own_strip, first_strip, probe, amplitude, light, matrix)
        received_change = move(send, spread)
        blocks = pltpu.VMEM((3, 2, height, LANES), jnp.float32)
        semaphores = pltpu.SemaphoreType.DMA((6,))
        updated, gradient, total, weight, first, second, others = call(
            base_kernel,
            (
                whole,
                whole,
                whole,
                shape(height, breadth),
                shape(height, frame),
                shape(height, frame),
                shape(8, LANES),
            ),
            [space(VMEM)] * 7 + [space(pl.ANY)],
            [space(pl.ANY)] * 2 + [space(VMEM)] * 5,
            [
                blocks,
                pltpu.VMEM((2, frame // LANES, frame + height, LANES), jnp.float32),
                pltpu.VMEM((2, frame, frame), jnp.float32),
                semaphores,
                pltpu.SemaphoreType.DMA((1,)),
            ],
            aliases={7: 1},
        )(place, found, swapped_found, staged, keep, light, plain, gradient)
        swapped_change = move(received_change, swap)
        updated, gradient = call(
            first_kernel,
            (whole, whole),
            [space(VMEM)] * 6 + [space(pl.ANY)] * 2,
            [space(pl.ANY)] * 2,
            [blocks, blocks, semaphores],
            aliases={6: 0, 7: 1},
        )(others, staged, total, weight, first, received_change, updated, gradient)
        return call(
            second_kernel,
            (whole, whole),
            [space(VMEM)] * 8 + [space(pl.ANY)] * 2,
            [space(pl.ANY)] * 2,
            [blocks, blocks, semaphores],
            aliases={8: 0, 9: 1},
        )(others, staged, total, weight, first, second, received_change, swapped_change, updated, gradient)

    return jax.shard_map(
        step,
        mesh=mesh,
        in_specs=(
            P(None, "tile", None),
            P("mode", None, None, None),
            P("tile", None, None),
            P(),
            P("tile"),
            P("tile"),
        ),
        out_specs=(P(None, "tile", None), P(None, "tile", None)),
        check_vma=False,
    )
```

profile of v0, /device:TPU:9, one launch (start us, length us, event | category | flops | bytes accessed | tf_op | source)
XLA Modules:
  0.0 45.2 jit_solution(3562110646115382037)
XLA Ops:
  0.7 0.7 %collective-permute-start.3 = (f32[2,128,2048]{2,1,0:T(8,128)}, f32[2,128,2048]{2,1,0:T(8,128)S(1)}, u32[]{:S(2)}, u32[]{:S(2)}) collective-permute-start(f32[2,128,2048]{2,1,0:T(8,128)} %param.7), channel_id=1, source_target_pairs={{0,1},{1,0},{2,3},{3,2},{4,5},{5,4},{6,7},{7,6},{8,9},{9,8},{10,11... | collective-permute-start | bytes 6291464 | tf_op jit(solution)/shard_map/ppermute | solution.py:475
  1.4 0.1 collective-permute-start.5
  1.5 0.4 collective-permute-start.2
  1.9 0.7 %collective-permute-start.8 = (f32[1,256,256]{2,1,0:T(8,128)}, f32[1,256,256]{2,1,0:T(8,128)S(1)}, u32[]{:S(2)}, u32[]{:S(2)}) collective-permute-start(f32[1,256,256]{2,1,0:T(8,128)} %own_ref.1), channel_id=1, source_target_pairs={{2,6},{6,10},{10,14},{14,18},{18,22},{22,26},{26,30}} | collective-permute-start | bytes 786440 | tf_op jit(solution)/shard_map/ppermute | solution.py:475
  2.6 3.1 %collective-permute-start.1 = (s32[1]{0:T(128)}, s32[1]{0:T(128)}, u32[]{:S(2)}, u32[]{:S(2)}) collective-permute-start(s32[1]{0:T(128)} %param.11), channel_id=1, source_target_pairs={{0,2},{2,4},{4,6},{6,8},{8,10},{10,12},{12,14},{14,16},{16,18},{18... | collective-permute-start | bytes 20 | tf_op jit(solution)/shard_map/ppermute | solution.py:475
  5.7 2.3 %collective-permute-done.1.scan_ref = s32[1]{0:T(128)} collective-permute-done((s32[1]{0:T(128)}, s32[1]{0:T(128)}, u32[]{:S(2)}, u32[]{:S(2)}) %collective-permute-start.1) | collective-permute-done | bytes 36 | tf_op jit(solution)/shard_map/ppermute | solution.py:475
  8.0 4.2 %collective-permute-start = (s32[1]{0:T(128)}, s32[1]{0:T(128)}, u32[]{:S(2)}, u32[]{:S(2)}) collective-permute-start(s32[1]{0:T(128)} %param.11), channel_id=1, source_target_pairs={{0,1},{1,0},{2,3},{3,2},{4,5},{5,4},{6,7},{7,6},{8,9},{9,8},{10,11... | collective-permute-start | bytes 20 | tf_op jit(solution)/shard_map/ppermute | solution.py:475
  12.2 1.1 %collective-permute-done.own_scan_ref = s32[1]{0:T(128)} collective-permute-done((s32[1]{0:T(128)}, s32[1]{0:T(128)}, u32[]{:S(2)}, u32[]{:S(2)}) %collective-permute-start) | collective-permute-done | bytes 36 | tf_op jit(solution)/shard_map/ppermute | solution.py:475
  13.3 0.0 collective-permute-done.2.table_ref
  13.3 0.0 collective-permute-done.3.object_ref
  13.3 1.4 %shard_map.77 = (f32[2,128,256]{2,1,0:T(8,128)S(1)}, f32[8,128]{1,0:T(8,128)S(1)}) custom-call(s32[1]{0:T(128)} %collective-permute-done.own_scan_ref, s32[1]{0:T(128)} %collective-permute-done.1.scan_ref, s32[2,8192]{1,0:T(2,128)S(1)} %collective-permute-done.2.table_ref, f32[2,128,2048]{2,1,0:T(8,128)S(1)} %collective-permute-done.3.object_ref), custom_call_target="tpu_custom_call" | custom-call | flops 5000000 | bytes 5000000 | tf_op jit(solution)/shard_map/pallas_call | solution.py:489
  14.8 1.9 %collective-permute-start.6 = (f32[2,128,256]{2,1,0:T(8,128)S(1)}, f32[2,128,256]{2,1,0:T(8,128)S(1)}, u32[]{:S(2)}, u32[]{:S(2)}) collective-permute-start(f32[2,128,256]{2,1,0:T(8,128)S(1)} %get-tuple-element.27), channel_id=1, source_target_pairs={{0,2},{2,0},{4,6},{6,4},{8,10},{10,8},{12,14},{14,12},{16,18},{18,... | collective-permute-start | bytes 786440 | tf_op jit(solution)/shard_map/ppermute | solution.py:475
  16.7 0.0 collective-permute-done.8.received_ref
  16.7 0.6 %collective-permute-start.9 = (f32[1,256,256]{2,1,0:T(8,128)S(1)}, f32[1,256,256]{2,1,0:T(8,128)S(1)}, u32[]{:S(2)}, u32[]{:S(2)}) collective-permute-start(f32[1,256,256]{2,1,0:T(8,128)S(1)} %collective-permute-done.8.received_ref), channel_id=1, source_target_pairs={{0,1},{1,0},{2,3},{3,2},{4,5},{5,4},{6,7},{7,6},{8,9},{9,8},{10,11... | collective-permute-start | bytes 786440 | tf_op jit(solution)/shard_map/ppermute | solution.py:475
  17.3 4.9 %collective-permute-done.6.received_ref = f32[2,128,256]{2,1,0:T(8,128)S(1)} collective-permute-done((f32[2,128,256]{2,1,0:T(8,128)S(1)}, f32[2,128,256]{2,1,0:T(8,128)S(1)}, u32[]{:S(2)}, u32[]{:S(2)}) %collective-permute-start.6) | collective-permute-done | bytes 262176 | tf_op jit(solution)/shard_map/ppermute | solution.py:475
  22.2 1.2 %collective-permute-start.7 = (f32[2,128,256]{2,1,0:T(8,128)S(1)}, f32[2,128,256]{2,1,0:T(8,128)S(1)}, u32[]{:S(2)}, u32[]{:S(2)}) collective-permute-start(f32[2,128,256]{2,1,0:T(8,128)S(1)} %collective-permute-done.6.received_ref), channel_id=1, source_target_pairs={{0,1},{1,0},{2,3},{3,2},{4,5},{5,4},{6,7},{7,6},{8,9},{9,8},{10,11... | collective-permute-start | bytes 786440 | tf_op jit(solution)/shard_map/ppermute | solution.py:475
  23.4 0.0 collective-permute-start.4
  23.4 0.0 collective-permute-done.9.swapped_ref
  23.4 0.3 shard_map.81.amplitude_ref
  23.7 1.4 %shard_map.78 = (f32[2,128,2048]{2,1,0:T(8,128)}, f32[256,256]{1,0:T(8,128)S(1)}) custom-call(f32[2,2,256,256]{3,2,1,0:T(8,128)S(1)} %copy-done, f32[2,2,256,256]{3,2,1,0:T(8,128)S(1)} %collective-permute-done.5.other_probe_ref), custom_call_target="tpu_custom_call" | custom-call | flops 5000000 | bytes 5000000 | tf_op jit(solution)/shard_map/pallas_call | solution.py:500
  25.2 0.0 copy-start.1
  25.2 1.0 %shard_map.79 = (f32[4,2,256,256]{3,2,1,0:T(8,128)S(1)}, f32[2,128,256]{2,1,0:T(8,128)S(1)}, f32[256,256]{1,0:T(8,128)S(1)}, f32[8,128]{1,0:T(8,128)S(1)}) custom-call(f32[8,128]{1,0:T(8,128)S(1)} %get-tuple-element.23.found_ref, f32[8,128]{1,0:T(8,128)S(1)} %collective-permute-done.4.swapped_ref, f32[2,128,2048]{2,1,0:T(8,128)S(1)} %collective-permute-done.3.object_ref, ...), custom_call_target="tpu_custom_call" | custom-call | flops 5000000 | bytes 5000000 | tf_op jit(solution)/shard_map/pallas_call | solution.py:507
  26.2 0.2 copy-done.1
  26.4 1.1 %shard_map.80 = (f32[4,2,128,256]{3,2,1,0:T(8,128)S(1)}, f32[4,2,128,256]{3,2,1,0:T(8,128)S(1)}) custom-call(f32[2,128,256]{2,1,0:T(8,128)S(1)} %get-tuple-element.26.own_ref.window_ref, f32[2,128,256]{2,1,0:T(8,128)S(1)} %collective-permute-done.6.received_ref, f32[4,2,256,256]{3,2,1,0:T(8,128)S(1)} %get-tuple-element.28.probe_ref, ...), custom_call_target="tpu_custom_call" | custom-call | flops 5000000 | bytes 5000000 | tf_op jit(solution)/shard_map/pallas_call | solution.py:527
  27.5 0.0 collective-permute-done.7.swapped_ref
  27.5 3.8 %shard_map.82 = (f32[264,256]{1,0:T(8,128)S(1)}, f32[2,128,256]{2,1,0:T(8,128)S(1)}) custom-call(f32[8,128]{1,0:T(8,128)S(1)} %get-tuple-element.25.place_ref, f32[2,128,256]{2,1,0:T(8,128)S(1)} %get-tuple-element.26.own_ref.window_ref, f32[2,128,256]{2,1,0:T(8,128)S(1)} %collective-permute-done.6.received_ref, ...), custom_call_target="tpu_custom_call" | custom-call | flops 5000000 | bytes 5000000 | tf_op jit(solution)/shard_map/pallas_call | solution.py:530
  31.3 2.0 %collective-permute-start.10 = (f32[264,256]{1,0:T(8,128)S(1)}, f32[264,256]{1,0:T(8,128)S(1)}, u32[]{:S(2)}, u32[]{:S(2)}) collective-permute-start(f32[264,256]{1,0:T(8,128)S(1)} %get-tuple-element.39), channel_id=1, source_target_pairs={{2,0},{0,2},{6,4},{4,6},{10,8},{8,10},{14,12},{12,14},{18,16},{16,... | collective-permute-start | bytes 811016 | tf_op jit(solution)/shard_map/ppermute | solution.py:475
  33.3 6.1 %collective-permute-done.10.received_ref = f32[264,256]{1,0:T(8,128)S(1)} collective-permute-done((f32[264,256]{1,0:T(8,128)S(1)}, f32[264,256]{1,0:T(8,128)S(1)}, u32[]{:S(2)}, u32[]{:S(2)}) %collective-permute-start.10) | collective-permute-done | bytes 270368 | tf_op jit(solution)/shard_map/ppermute | solution.py:475
  39.4 0.8 %collective-permute-start.11 = (f32[264,256]{1,0:T(8,128)S(1)}, f32[264,256]{1,0:T(8,128)S(1)}, u32[]{:S(2)}, u32[]{:S(2)}) collective-permute-start(f32[264,256]{1,0:T(8,128)S(1)} %collective-permute-done.10.received_ref), channel_id=1, source_target_pairs={{0,1},{1,0},{2,3},{3,2},{4,5},{5,4},{6,7},{7,6},{8,9},{9,8},{10,11... | collective-permute-start | bytes 811016 | tf_op jit(solution)/shard_map/ppermute | solution.py:475
  40.2 2.6 %shard_map.83 = (f32[2,128,2048]{2,1,0:T(8,128)}, f32[2,128,2048]{2,1,0:T(8,128)}, f32[2,128,2048]{2,1,0:T(8,128)S(1)}, f32[128,2048]{1,0:T(8,128)S(1)}, f32[128...) custom-call(f32[8,128]{1,0:T(8,128)S(1)} %get-tuple-element.25.place_ref, ...), custom_call_target="tpu_custom_call", output_to_operand_aliasing={{1}: (7, {})} | custom-call | flops 5000000 | bytes 5000000 | tf_op jit(solution)/shard_map/pallas_call | solution.py:545
  42.8 1.1 %shard_map.84 = (f32[2,128,2048]{2,1,0:T(8,128)}, f32[2,128,2048]{2,1,0:T(8,128)}) custom-call(f32[8,128]{1,0:T(8,128)S(1)} %get-tuple-element.34.others_ref, f32[2,128,2048]{2,1,0:T(8,128)S(1)} %collective-permute-done.3.object_ref, f32[2,128,2048]{2,1,0:T(8,128)S(1)} %get-tuple-element.35.total_ref, ...), custom_call_target="tpu_custom_call", output_to_operand_aliasing={{0}: (6, {}), {1}: (7, {})} | custom-call | flops 5000000 | bytes 5000000 | tf_op jit(solution)/shard_map/pallas_call | solution.py:568
  44.0 1.2 %shard_map.85 = (f32[2,128,2048]{2,1,0:T(8,128)}, f32[2,128,2048]{2,1,0:T(8,128)}) custom-call(f32[8,128]{1,0:T(8,128)S(1)} %get-tuple-element.34.others_ref, f32[2,128,2048]{2,1,0:T(8,128)S(1)} %collective-permute-done.3.object_ref, f32[2,128,2048]{2,1,0:T(8,128)S(1)} %get-tuple-element.35.total_ref, ...), custom_call_target="tpu_custom_call", output_to_operand_aliasing={{0}: (8, {}), {1}: (9, {})} | custom-call | flops 5000000 | bytes 5000000 | tf_op jit(solution)/shard_map/pallas_call | solution.py:576
  (7 shorter events, 0.0 us)
Async XLA Ops:
  0.6 23.1 %copy-start = (f32[2,2,256,256]{3,2,1,0:T(8,128)S(1)}, f32[2,2,256,256]{3,2,1,0:T(8,128)}, u32[]{:S(2)}) copy-start(f32[2,2,256,256]{3,2,1,0:T(8,128)} %own_probe_ref.3) | copy-start | bytes 3145732
  0.6 22.8 %copy-start.2 = (f32[1,256,256]{2,1,0:T(8,128)S(1)}, f32[1,256,256]{2,1,0:T(8,128)}, u32[]{:S(2)}) copy-start(f32[1,256,256]{2,1,0:T(8,128)} %own_ref.1) | copy-start | bytes 786436
  0.7 12.7 %collective-permute-start.3 = (f32[2,128,2048]{2,1,0:T(8,128)}, f32[2,128,2048]{2,1,0:T(8,128)S(1)}, u32[]{:S(2)}, u32[]{:S(2)}) collective-permute-start(f32[2,128,2048]{2,1,0:T(8,128)} %param.7), channel_id=1, source_target_pairs={{0,1},{1,0},{2,3},{3,2},{4,5},{5,4},{6,7},{7,6},{8,9},{9,8},{10,11... | collective-permute-start | bytes 6291464 | tf_op jit(solution)/shard_map/ppermute | solution.py:475
  1.4 22.3 %collective-permute-start.5 = (f32[2,2,256,256]{3,2,1,0:T(8,128)}, f32[2,2,256,256]{3,2,1,0:T(8,128)S(1)}, u32[]{:S(2)}, u32[]{:S(2)}) collective-permute-start(f32[2,2,256,256]{3,2,1,0:T(8,128)} %own_probe_ref.3), channel_id=1, source_target_pairs={{0,1},{1,0},{2,3},{3,2},{4,5},{5,4},{6,7},{7,6},{8,9},{9,8},{10,11... | collective-permute-start | bytes 3145736 | tf_op jit(solution)/shard_map/ppermute | solution.py:475
  1.5 11.9 %collective-permute-start.2 = (s32[2,8192]{1,0:T(2,128)}, s32[2,8192]{1,0:T(2,128)S(1)}, u32[]{:S(2)}, u32[]{:S(2)}) collective-permute-start(s32[2,8192]{1,0:T(2,128)} %bitcast.1), channel_id=1, source_target_pairs={{0,1},{1,0},{2,3},{3,2},{4,5},{5,4},{6,7},{7,6},{8,9},{9,8},{10,11... | collective-permute-start | bytes 196616 | tf_op jit(solution)/shard_map/ppermute | solution.py:475
  1.9 14.8 %collective-permute-start.8 = (f32[1,256,256]{2,1,0:T(8,128)}, f32[1,256,256]{2,1,0:T(8,128)S(1)}, u32[]{:S(2)}, u32[]{:S(2)}) collective-permute-start(f32[1,256,256]{2,1,0:T(8,128)} %own_ref.1), channel_id=1, source_target_pairs={{2,6},{6,10},{10,14},{14,18},{18,22},{22,26},{26,30}} | collective-permute-start | bytes 786440 | tf_op jit(solution)/shard_map/ppermute | solution.py:475
  2.6 5.5 %collective-permute-start.1 = (s32[1]{0:T(128)}, s32[1]{0:T(128)}, u32[]{:S(2)}, u32[]{:S(2)}) collective-permute-start(s32[1]{0:T(128)} %param.11), channel_id=1, source_target_pairs={{0,2},{2,4},{4,6},{6,8},{8,10},{10,12},{12,14},{14,16},{16,18},{18... | collective-permute-start | bytes 20 | tf_op jit(solution)/shard_map/ppermute | solution.py:475
  8.0 5.3 %collective-permute-start = (s32[1]{0:T(128)}, s32[1]{0:T(128)}, u32[]{:S(2)}, u32[]{:S(2)}) collective-permute-start(s32[1]{0:T(128)} %param.11), channel_id=1, source_target_pairs={{0,1},{1,0},{2,3},{3,2},{4,5},{5,4},{6,7},{7,6},{8,9},{9,8},{10,11... | collective-permute-start | bytes 20 | tf_op jit(solution)/shard_map/ppermute | solution.py:475
  14.8 7.4 %collective-permute-start.6 = (f32[2,128,256]{2,1,0:T(8,128)S(1)}, f32[2,128,256]{2,1,0:T(8,128)S(1)}, u32[]{:S(2)}, u32[]{:S(2)}) collective-permute-start(f32[2,128,256]{2,1,0:T(8,128)S(1)} %get-tuple-element.27), channel_id=1, source_target_pairs={{0,2},{2,0},{4,6},{6,4},{8,10},{10,8},{12,14},{14,12},{16,18},{18,... | collective-permute-start | bytes 786440 | tf_op jit(solution)/shard_map/ppermute | solution.py:475
  16.7 6.7 %collective-permute-start.9 = (f32[1,256,256]{2,1,0:T(8,128)S(1)}, f32[1,256,256]{2,1,0:T(8,128)S(1)}, u32[]{:S(2)}, u32[]{:S(2)}) collective-permute-start(f32[1,256,256]{2,1,0:T(8,128)S(1)} %collective-permute-done.8.received_ref), channel_id=1, source_target_pairs={{0,1},{1,0},{2,3},{3,2},{4,5},{5,4},{6,7},{7,6},{8,9},{9,8},{10,11... | collective-permute-start | bytes 786440 | tf_op jit(solution)/shard_map/ppermute | solution.py:475
  22.2 5.3 %collective-permute-start.7 = (f32[2,128,256]{2,1,0:T(8,128)S(1)}, f32[2,128,256]{2,1,0:T(8,128)S(1)}, u32[]{:S(2)}, u32[]{:S(2)}) collective-permute-start(f32[2,128,256]{2,1,0:T(8,128)S(1)} %collective-permute-done.6.received_ref), channel_id=1, source_target_pairs={{0,1},{1,0},{2,3},{3,2},{4,5},{5,4},{6,7},{7,6},{8,9},{9,8},{10,11... | collective-permute-start | bytes 786440 | tf_op jit(solution)/shard_map/ppermute | solution.py:475
  23.4 1.8 %collective-permute-start.4 = (f32[8,128]{1,0:T(8,128)S(1)}, f32[8,128]{1,0:T(8,128)S(1)}, u32[]{:S(2)}, u32[]{:S(2)}) collective-permute-start(f32[8,128]{1,0:T(8,128)S(1)} %get-tuple-element.23.found_ref), channel_id=1, source_target_pairs={{0,1},{1,0},{2,3},{3,2},{4,5},{5,4},{6,7},{7,6},{8,9},{9,8},{10,11... | collective-permute-start | bytes 12296 | tf_op jit(solution)/shard_map/ppermute | solution.py:475
  25.2 1.2 %copy-start.1 = (bf16[8,256,256]{2,1,0:T(8,128)(2,1)S(1)}, bf16[8,256,256]{2,1,0:T(8,128)(2,1)}, u32[]{:S(2)}) copy-start(bf16[8,256,256]{2,1,0:T(8,128)(2,1)} %constant.2.clone.matrix_ref) | copy-start | bytes 3145732
  31.3 8.1 %collective-permute-start.10 = (f32[264,256]{1,0:T(8,128)S(1)}, f32[264,256]{1,0:T(8,128)S(1)}, u32[]{:S(2)}, u32[]{:S(2)}) collective-permute-start(f32[264,256]{1,0:T(8,128)S(1)} %get-tuple-element.39), channel_id=1, source_target_pairs={{2,0},{0,2},{6,4},{4,6},{10,8},{8,10},{14,12},{12,14},{18,16},{16,... | collective-permute-start | bytes 811016 | tf_op jit(solution)/shard_map/ppermute | solution.py:475
  39.4 4.5 %collective-permute-start.11 = (f32[264,256]{1,0:T(8,128)S(1)}, f32[264,256]{1,0:T(8,128)S(1)}, u32[]{:S(2)}, u32[]{:S(2)}) collective-permute-start(f32[264,256]{1,0:T(8,128)S(1)} %collective-permute-done.10.received_ref), channel_id=1, source_target_pairs={{0,1},{1,0},{2,3},{3,2},{4,5},{5,4},{6,7},{7,6},{8,9},{9,8},{10,11... | collective-permute-start | bytes 811016 | tf_op jit(solution)/shard_map/ppermute | solution.py:475
where the time goes:
time: 45.5 us; the launch traced here: 45.2 us
  starting transfers between devices  15.7 us (35%)
  waiting for transfers between devices  14.4 us (32%)
  Pallas kernels  14.1 us (31%)
  between operations  0.8 us (2%)
    ppermute x12, starting transfers between devices, move(): return lax.ppermute(value, AXES, pairs)  15.7 us
    ppermute x12, waiting for transfers between devices, move(): return lax.ppermute(value, AXES, pairs)  14.4 us
    pallas_call x1, Pallas kernels, step(): call(wave_kernel, (shape(2 * height + 8, frame), shape(2, height, frame))...  3.82 us
    pallas_call x1, Pallas kernels, step(): call(base_kernel, (whole, whole, whole, shape(height, breadth), shape(hei...  2.59 us
    pallas_call x1, Pallas kernels, step(): call(select_kernel, (shape(2, height, frame), shape(8, LANES)), [space(SM...  1.45 us
    pallas_call x1, Pallas kernels, step(): call(fill_kernel, (whole, shape(frame, frame)), [space(VMEM)] * 2, [space...  1.45 us
    pallas_call x1, Pallas kernels, step(): call(second_kernel, (whole, whole), [space(VMEM)] * 8 + [space(pl.ANY)] *...  1.25 us
    pallas_call x1, Pallas kernels, step(): call(first_kernel, (whole, whole), [space(VMEM)] * 6 + [space(pl.ANY)] *...  1.13 us
  transfers between devices with their start and end apart: 12, of which 4 were waited for; matrix products, arithmetic and copies ran while one was open for 0% of the time, Pallas kernels for 20%

commit v1 on v0

--- a/solution.py
+++ b/solution.py
@@ -160,8 +160,8 @@
 
 
 def prepare_kernel(
-    found_ref, swapped_ref, object_ref, own_probe_ref, other_probe_ref, total_ref,
-    probe_ref, window_ref, light_ref, place_ref, tall_ref,
+    found_ref, swapped_ref, object_ref, own_probe_ref, other_probe_ref, total_ref, matrix_ref,
+    probe_ref, window_ref, light_ref, place_ref, strip_ref, tall_ref,
 ):
     sources = probe_parts(own_probe_ref, other_probe_ref)
     height = object_ref.shape[1]
@@ -178,6 +178,7 @@
     window_ref[:, :, LANES:] = high
     live = jnp.where(odd == 1, (tile >= 2).astype(jnp.int32), 1)
     keep_scalars(place_ref, (jnp.where(odd == 1, 0, row), jnp.where(odd == 1, row, height), live))
+    transform_rows(probe_ref, 0, window_ref, matrix_ref, strip_ref)
 
 
 def right(value, high, low):
@@ -223,10 +224,9 @@
         out_ref[mode, 1] = jnp.concatenate([even[at, half:], odd[at, half:]], axis=1)
 
 
-def strip_kernel(own_ref, received_ref, probe_ref, matrix_ref, own_out_ref, out_ref):
+def strip_kernel(received_ref, probe_ref, matrix_ref, out_ref):
     height = received_ref.shape[1]
     start = pl.multiple_of((1 - lax.axis_index("mode")) * height, height)
-    transform_rows(probe_ref, 0, own_ref, matrix_ref, own_out_ref)
     transform_rows(probe_ref, start, received_ref, matrix_ref, out_ref)
 
 
@@ -483,7 +483,6 @@
         received_scan = move(slot_scan, up)
         staged = move(object_tiles, swap)
         table = move(table, swap)
-        own_scan = move(slot_scan, swap)
         other_probe = move(probe_modes, swap)
         received_amplitude = move(amplitudes, onward)
         window, found = call(
@@ -491,7 +490,7 @@
             (shape(2, height, frame), shape(8, LANES)),
             [space(SMEM)] * 2 + [space(VMEM)] * 2,
             [space(VMEM)] * 2,
-        )(own_scan, received_scan, table, staged)
+        )(slot_scan, received_scan, table, staged)
         received = move(window, gather)
         swapped_found = move(found, swap)
         swapped_amplitude = move(received_amplitude, swap)
@@ -504,18 +503,19 @@
             [space(pl.ANY), space(VMEM)],
             [pltpu.VMEM((height // 8, breadth), jnp.float32), pltpu.SemaphoreType.DMA((16,))],
         )(probe_modes, other_probe)
-        probe, own_window, light, place = call(
+        probe, own_window, light, place, own_strip = call(
             prepare_kernel,
             (
                 shape(2 * modes, 2, frame, frame),
                 shape(2, height, frame),
                 shape(frame, frame),
                 shape(8, LANES),
+                strip,
             ),
-            [space(VMEM)] * 6,
-            [space(VMEM)] * 4,
+            [space(VMEM)] * 7,
+            [space(VMEM)] * 5,
             [pltpu.VMEM((4 * modes + 1, frame // LANES, frame + height, LANES), jnp.float32)],
-        )(found, swapped_found, staged, probe_modes, other_probe, plain)
+        )(found, swapped_found, staged, probe_modes, other_probe, plain, matrix)
         swapped = move(received, swap)
         amplitude = call(
             reorder_kernel,
@@ -524,9 +524,7 @@
             space(VMEM),
             [pltpu.VMEM((frame // LANES, frame, LANES), jnp.float32)],
         )(amplitudes, received_amplitude, swapped_amplitude)
-        own_strip, first_strip = call(strip_kernel, (strip, strip), [space(VMEM)] * 4, [space(VMEM)] * 2)(
-            own_window, received, probe, matrix
-        )
+        first_strip = call(strip_kernel, strip, [space(VMEM)] * 3, space(VMEM))(received, probe, matrix)
         send, keep = call(
             wave_kernel,
             (shape(2 * height + 8, frame), shape(2, height, frame)),

time: 45.5 us -> 43.8 us (0.963)
  waiting for transfers between devices: 14.4 us -> 8.54 us
  starting transfers between devices: 15.7 us -> 19.6 us
  between operations: 0.8 us -> 1.47 us
    ppermute x12 -> x11, waiting for transfers between devices: 14.4 us -> 8.54 us  [move(): return lax.ppermute(value, AXES, pairs)]
    ppermute x12 -> x11, starting transfers between devices: 15.7 us -> 19.6 us  [move(): return lax.ppermute(value, AXES, pairs)]
    pallas_call x1, Pallas kernels: 0.98 us -> 1.67 us  [step(): call(prepare_kernel, (shape(2 * modes, 2, frame, frame), shape(2, height,...]
    pallas_call x1, Pallas kernels: 1.45 us -> 0.89 us  [step(): call(select_kernel, (shape(2, height, frame), shape(8, LANES)), [space(SM...]
  transfers between devices with their start and end apart: 12 -> 11, of which waited for: 4 -> 3; matrix products, arithmetic and copies ran while one was open for 0% -> 0% of each run, Pallas kernels for 20% -> 20%
where the time goes in v1:
time: 43.8 us; the launch traced here: 43.6 us
  starting transfers between devices  19.6 us (45%)
  Pallas kernels  13.9 us (32%)
  waiting for transfers between devices  8.54 us (19%)
  between operations  1.47 us (3%)
    ppermute x11, starting transfers between devices, move(): return lax.ppermute(value, AXES, pairs)  19.6 us
    ppermute x11, waiting for transfers between devices, move(): return lax.ppermute(value, AXES, pairs)  8.54 us
    pallas_call x1, Pallas kernels, step(): call(wave_kernel, (shape(2 * height + 8, frame), shape(2, height, frame))...  4 us
    pallas_call x1, Pallas kernels, step(): call(base_kernel, (whole, whole, whole, shape(height, breadth), shape(hei...  2.6 us
    pallas_call x1, Pallas kernels, step(): call(prepare_kernel, (shape(2 * modes, 2, frame, frame), shape(2, height,...  1.67 us
    pallas_call x1, Pallas kernels, step(): call(fill_kernel, (whole, shape(frame, frame)), [space(VMEM)] * 2, [space...  1.45 us
    pallas_call x1, Pallas kernels, step(): call(second_kernel, (whole, whole), [space(VMEM)] * 8 + [space(pl.ANY)] *...  1.25 us
    pallas_call x1, Pallas kernels, step(): call(first_kernel, (whole, whole), [space(VMEM)] * 6 + [space(pl.ANY)] *...  1.13 us
  transfers between devices with their start and end apart: 11, of which 3 were waited for; matrix products, arithmetic and copies ran while one was open for 0% of the time, Pallas kernels for 20%

profile of v1, /device:TPU:9, one launch (start us, length us, event | category | flops | bytes accessed | tf_op | source)
XLA Modules:
  0.0 43.6 jit_solution(8412690277073152654)
XLA Ops:
  0.7 0.7 %collective-permute-start.2 = (f32[2,128,2048]{2,1,0:T(8,128)}, f32[2,128,2048]{2,1,0:T(8,128)S(1)}, u32[]{:S(2)}, u32[]{:S(2)}) collective-permute-start(f32[2,128,2048]{2,1,0:T(8,128)} %param.7), channel_id=1, source_target_pairs={{0,1},{1,0},{2,3},{3,2},{4,5},{5,4},{6,7},{7,6},{8,9},{9,8},{10,11... | collective-permute-start | bytes 6291464 | tf_op jit(solution)/shard_map/ppermute | solution.py:475
  1.4 0.1 collective-permute-start.4
  1.5 0.4 collective-permute-start.1
  1.9 0.7 %collective-permute-start.7 = (f32[1,256,256]{2,1,0:T(8,128)}, f32[1,256,256]{2,1,0:T(8,128)S(1)}, u32[]{:S(2)}, u32[]{:S(2)}) collective-permute-start(f32[1,256,256]{2,1,0:T(8,128)} %own_ref.1), channel_id=1, source_target_pairs={{2,6},{6,10},{10,14},{14,18},{18,22},{22,26},{26,30}} | collective-permute-start | bytes 786440 | tf_op jit(solution)/shard_map/ppermute | solution.py:475
  2.6 3.1 %collective-permute-start = (s32[1]{0:T(128)}, s32[1]{0:T(128)}, u32[]{:S(2)}, u32[]{:S(2)}) collective-permute-start(s32[1]{0:T(128)} %param.11), channel_id=1, source_target_pairs={{0,2},{2,4},{4,6},{6,8},{8,10},{10,12},{12,14},{14,16},{16,18},{18... | collective-permute-start | bytes 20 | tf_op jit(solution)/shard_map/ppermute | solution.py:475
  6.4 1.6 %collective-permute-done.scan_ref = s32[1]{0:T(128)} collective-permute-done((s32[1]{0:T(128)}, s32[1]{0:T(128)}, u32[]{:S(2)}, u32[]{:S(2)}) %collective-permute-start) | collective-permute-done | bytes 36 | tf_op jit(solution)/shard_map/ppermute | solution.py:475
  8.0 0.0 collective-permute-done.1.table_ref
  8.0 0.0 collective-permute-done.2.object_ref
  8.0 0.9 %shard_map.77 = (f32[2,128,256]{2,1,0:T(8,128)S(1)}, f32[8,128]{1,0:T(8,128)S(1)}) custom-call(s32[1]{0:T(128)S(6)} %copy.18.own_scan_ref, s32[1]{0:T(128)} %collective-permute-done.scan_ref, s32[2,8192]{1,0:T(2,128)S(1)} %collective-permute-done.1.table_ref, f32[2,128,2048]{2,1,0:T(8,128)S(1)} %collective-permute-done.2.object_ref), custom_call_target="tpu_custom_call" | custom-call | flops 5000000 | bytes 5000000 | tf_op jit(solution)/shard_map/pallas_call | solution.py:488
  8.9 0.0 copy-start
  8.9 2.3 %collective-permute-start.5 = (f32[2,128,256]{2,1,0:T(8,128)S(1)}, f32[2,128,256]{2,1,0:T(8,128)S(1)}, u32[]{:S(2)}, u32[]{:S(2)}) collective-permute-start(f32[2,128,256]{2,1,0:T(8,128)S(1)} %get-tuple-element.26), channel_id=1, source_target_pairs={{0,2},{2,0},{4,6},{6,4},{8,10},{10,8},{12,14},{14,12},{16,18},{18,... | collective-permute-start | bytes 786440 | tf_op jit(solution)/shard_map/ppermute | solution.py:475
  11.2 0.0 collective-permute-done.7.received_ref
  11.2 4.3 %collective-permute-start.8 = (f32[1,256,256]{2,1,0:T(8,128)S(1)}, f32[1,256,256]{2,1,0:T(8,128)S(1)}, u32[]{:S(2)}, u32[]{:S(2)}) collective-permute-start(f32[1,256,256]{2,1,0:T(8,128)S(1)} %collective-permute-done.7.received_ref), channel_id=1, source_target_pairs={{0,1},{1,0},{2,3},{3,2},{4,5},{5,4},{6,7},{7,6},{8,9},{9,8},{10,11... | collective-permute-start | bytes 786440 | tf_op jit(solution)/shard_map/ppermute | solution.py:475
  15.5 0.7 %collective-permute-done.5.received_ref = f32[2,128,256]{2,1,0:T(8,128)S(1)} collective-permute-done((f32[2,128,256]{2,1,0:T(8,128)S(1)}, f32[2,128,256]{2,1,0:T(8,128)S(1)}, u32[]{:S(2)}, u32[]{:S(2)}) %collective-permute-start.5) | collective-permute-done | bytes 262176 | tf_op jit(solution)/shard_map/ppermute | solution.py:475
  16.2 5.4 %collective-permute-start.6 = (f32[2,128,256]{2,1,0:T(8,128)S(1)}, f32[2,128,256]{2,1,0:T(8,128)S(1)}, u32[]{:S(2)}, u32[]{:S(2)}) collective-permute-start(f32[2,128,256]{2,1,0:T(8,128)S(1)} %collective-permute-done.5.received_ref), channel_id=1, source_target_pairs={{0,1},{1,0},{2,3},{3,2},{4,5},{5,4},{6,7},{7,6},{8,9},{9,8},{10,11... | collective-permute-start | bytes 786440 | tf_op jit(solution)/shard_map/ppermute | solution.py:475
  21.5 0.0 collective-permute-start.3
  21.6 0.0 collective-permute-done.8.swapped_ref
  21.6 0.3 shard_map.81.amplitude_ref
  21.9 0.0 collective-permute-done.4.other_probe_ref
  21.9 1.4 %shard_map.78 = (f32[2,128,2048]{2,1,0:T(8,128)}, f32[256,256]{1,0:T(8,128)S(1)}) custom-call(f32[2,2,256,256]{3,2,1,0:T(8,128)S(1)} %copy-done.1, f32[2,2,256,256]{3,2,1,0:T(8,128)S(1)} %collective-permute-done.4.other_probe_ref), custom_call_target="tpu_custom_call" | custom-call | flops 5000000 | bytes 5000000 | tf_op jit(solution)/shard_map/pallas_call | solution.py:499
  23.3 0.0 collective-permute-done.3.swapped_ref
  23.4 1.7 %shard_map.79 = (f32[4,2,256,256]{3,2,1,0:T(8,128)S(1)}, f32[2,128,256]{2,1,0:T(8,128)S(1)}, f32[256,256]{1,0:T(8,128)S(1)}, f32[8,128]{1,0:T(8,128)S(1)}, f32[4,2,128,256]{3,2,1,0:T(8,128)S(1)}) custom-call(f32[8,128]{1,0:T(8,128)S(1)} %get-tuple-element.22.found_ref, f32[8,128]{1,0:T(8,128)S(1)} %collective-permute-done.3.swapped_ref, ...), custom_call_target="tpu_custom_call" | custom-call | flops 5000000 | bytes 5000000 | tf_op jit(solution)/shard_map/pallas_call | solution.py:506
  25.0 0.6 %shard_map.80.first_ref = f32[4,2,128,256]{3,2,1,0:T(8,128)S(1)} custom-call(f32[2,128,256]{2,1,0:T(8,128)S(1)} %collective-permute-done.5.received_ref, f32[4,2,256,256]{3,2,1,0:T(8,128)S(1)} %get-tuple-element.28.probe_ref, bf16[8,256,256]{2,1,0:T(8,128)(2,1)S(1)} %copy-done), custom_call_target="tpu_custom_call" | custom-call | flops 5000000 | bytes 5000000 | tf_op jit(solution)/shard_map/pallas_call | solution.py:527
  25.7 0.0 collective-permute-done.6.swapped_ref
  25.7 4.0 %shard_map.82 = (f32[264,256]{1,0:T(8,128)S(1)}, f32[2,128,256]{2,1,0:T(8,128)S(1)}) custom-call(f32[8,128]{1,0:T(8,128)S(1)} %get-tuple-element.24.place_ref, f32[2,128,256]{2,1,0:T(8,128)S(1)} %get-tuple-element.25.window_ref, f32[2,128,256]{2,1,0:T(8,128)S(1)} %collective-permute-done.5.received_ref, ...), custom_call_target="tpu_custom_call" | custom-call | flops 5000000 | bytes 5000000 | tf_op jit(solution)/shard_map/pallas_call | solution.py:528
  29.7 1.9 %collective-permute-start.9 = (f32[264,256]{1,0:T(8,128)S(1)}, f32[264,256]{1,0:T(8,128)S(1)}, u32[]{:S(2)}, u32[]{:S(2)}) collective-permute-start(f32[264,256]{1,0:T(8,128)S(1)} %get-tuple-element.37), channel_id=1, source_target_pairs={{2,0},{0,2},{6,4},{4,6},{10,8},{8,10},{14,12},{12,14},{18,16},{16,... | collective-permute-start | bytes 811016 | tf_op jit(solution)/shard_map/ppermute | solution.py:475
  31.6 6.2 %collective-permute-done.9.received_ref = f32[264,256]{1,0:T(8,128)S(1)} collective-permute-done((f32[264,256]{1,0:T(8,128)S(1)}, f32[264,256]{1,0:T(8,128)S(1)}, u32[]{:S(2)}, u32[]{:S(2)}) %collective-permute-start.9) | collective-permute-done | bytes 270368 | tf_op jit(solution)/shard_map/ppermute | solution.py:475
  37.8 0.8 %collective-permute-start.10 = (f32[264,256]{1,0:T(8,128)S(1)}, f32[264,256]{1,0:T(8,128)S(1)}, u32[]{:S(2)}, u32[]{:S(2)}) collective-permute-start(f32[264,256]{1,0:T(8,128)S(1)} %collective-permute-done.9.received_ref), channel_id=1, source_target_pairs={{0,1},{1,0},{2,3},{3,2},{4,5},{5,4},{6,7},{7,6},{8,9},{9,8},{10,11... | collective-permute-start | bytes 811016 | tf_op jit(solution)/shard_map/ppermute | solution.py:475
  38.5 2.6 %shard_map.83 = (f32[2,128,2048]{2,1,0:T(8,128)}, f32[2,128,2048]{2,1,0:T(8,128)}, f32[2,128,2048]{2,1,0:T(8,128)S(1)}, f32[128,2048]{1,0:T(8,128)S(1)}, f32[128...) custom-call(f32[8,128]{1,0:T(8,128)S(1)} %get-tuple-element.24.place_ref, ...), custom_call_target="tpu_custom_call", output_to_operand_aliasing={{1}: (7, {})} | custom-call | flops 5000000 | bytes 5000000 | tf_op jit(solution)/shard_map/pallas_call | solution.py:543
  41.2 1.1 %shard_map.84 = (f32[2,128,2048]{2,1,0:T(8,128)}, f32[2,128,2048]{2,1,0:T(8,128)}) custom-call(f32[8,128]{1,0:T(8,128)S(1)} %get-tuple-element.32.others_ref, f32[2,128,2048]{2,1,0:T(8,128)S(1)} %collective-permute-done.2.object_ref, f32[2,128,2048]{2,1,0:T(8,128)S(1)} %get-tuple-element.33.total_ref, ...), custom_call_target="tpu_custom_call", output_to_operand_aliasing={{0}: (6, {}), {1}: (7, {})} | custom-call | flops 5000000 | bytes 5000000 | tf_op jit(solution)/shard_map/pallas_call | solution.py:566
  42.3 0.0 collective-permute-done.10.swapped_ref
  42.3 1.2 %shard_map.85 = (f32[2,128,2048]{2,1,0:T(8,128)}, f32[2,128,2048]{2,1,0:T(8,128)}) custom-call(f32[8,128]{1,0:T(8,128)S(1)} %get-tuple-element.32.others_ref, f32[2,128,2048]{2,1,0:T(8,128)S(1)} %collective-permute-done.2.object_ref, f32[2,128,2048]{2,1,0:T(8,128)S(1)} %get-tuple-element.33.total_ref, ...), custom_call_target="tpu_custom_call", output_to_operand_aliasing={{0}: (8, {}), {1}: (9, {})} | custom-call | flops 5000000 | bytes 5000000 | tf_op jit(solution)/shard_map/pallas_call | solution.py:574
  (5 shorter events, 0.0 us)
Async XLA Ops:
  0.6 21.2 %copy-start.1 = (f32[2,2,256,256]{3,2,1,0:T(8,128)S(1)}, f32[2,2,256,256]{3,2,1,0:T(8,128)}, u32[]{:S(2)}) copy-start(f32[2,2,256,256]{3,2,1,0:T(8,128)} %own_probe_ref.3) | copy-start | bytes 3145732
  0.6 20.9 %copy-start.2 = (f32[1,256,256]{2,1,0:T(8,128)S(1)}, f32[1,256,256]{2,1,0:T(8,128)}, u32[]{:S(2)}) copy-start(f32[1,256,256]{2,1,0:T(8,128)} %own_ref.1) | copy-start | bytes 786436
  0.7 7.4 %collective-permute-start.2 = (f32[2,128,2048]{2,1,0:T(8,128)}, f32[2,128,2048]{2,1,0:T(8,128)S(1)}, u32[]{:S(2)}, u32[]{:S(2)}) collective-permute-start(f32[2,128,2048]{2,1,0:T(8,128)} %param.7), channel_id=1, source_target_pairs={{0,1},{1,0},{2,3},{3,2},{4,5},{5,4},{6,7},{7,6},{8,9},{9,8},{10,11... | collective-permute-start | bytes 6291464 | tf_op jit(solution)/shard_map/ppermute | solution.py:475
  1.4 20.5 %collective-permute-start.4 = (f32[2,2,256,256]{3,2,1,0:T(8,128)}, f32[2,2,256,256]{3,2,1,0:T(8,128)S(1)}, u32[]{:S(2)}, u32[]{:S(2)}) collective-permute-start(f32[2,2,256,256]{3,2,1,0:T(8,128)} %own_probe_ref.3), channel_id=1, source_target_pairs={{0,1},{1,0},{2,3},{3,2},{4,5},{5,4},{6,7},{7,6},{8,9},{9,8},{10,11... | collective-permute-start | bytes 3145736 | tf_op jit(solution)/shard_map/ppermute | solution.py:475
  1.5 6.6 %collective-permute-start.1 = (s32[2,8192]{1,0:T(2,128)}, s32[2,8192]{1,0:T(2,128)S(1)}, u32[]{:S(2)}, u32[]{:S(2)}) collective-permute-start(s32[2,8192]{1,0:T(2,128)} %bitcast.1), channel_id=1, source_target_pairs={{0,1},{1,0},{2,3},{3,2},{4,5},{5,4},{6,7},{7,6},{8,9},{9,8},{10,11... | collective-permute-start | bytes 196616 | tf_op jit(solution)/shard_map/ppermute | solution.py:475
  1.9 9.3 %collective-permute-start.7 = (f32[1,256,256]{2,1,0:T(8,128)}, f32[1,256,256]{2,1,0:T(8,128)S(1)}, u32[]{:S(2)}, u32[]{:S(2)}) collective-permute-start(f32[1,256,256]{2,1,0:T(8,128)} %own_ref.1), channel_id=1, source_target_pairs={{2,6},{6,10},{10,14},{14,18},{18,22},{22,26},{26,30}} | collective-permute-start | bytes 786440 | tf_op jit(solution)/shard_map/ppermute | solution.py:475
  2.6 5.5 %collective-permute-start = (s32[1]{0:T(128)}, s32[1]{0:T(128)}, u32[]{:S(2)}, u32[]{:S(2)}) collective-permute-start(s32[1]{0:T(128)} %param.11), channel_id=1, source_target_pairs={{0,2},{2,4},{4,6},{6,8},{8,10},{10,12},{12,14},{14,16},{16,18},{18... | collective-permute-start | bytes 20 | tf_op jit(solution)/shard_map/ppermute | solution.py:475
  8.9 14.4 %copy-start = (bf16[8,256,256]{2,1,0:T(8,128)(2,1)S(1)}, bf16[8,256,256]{2,1,0:T(8,128)(2,1)}, u32[]{:S(2)}) copy-start(bf16[8,256,256]{2,1,0:T(8,128)(2,1)} %constant.2.clone.matrix_ref) | copy-start | bytes 3145732
  8.9 7.2 %collective-permute-start.5 = (f32[2,128,256]{2,1,0:T(8,128)S(1)}, f32[2,128,256]{2,1,0:T(8,128)S(1)}, u32[]{:S(2)}, u32[]{:S(2)}) collective-permute-start(f32[2,128,256]{2,1,0:T(8,128)S(1)} %get-tuple-element.26), channel_id=1, source_target_pairs={{0,2},{2,0},{4,6},{6,4},{8,10},{10,8},{12,14},{14,12},{16,18},{18,... | collective-permute-start | bytes 786440 | tf_op jit(solution)/shard_map/ppermute | solution.py:475
  11.2 10.3 %collective-permute-start.8 = (f32[1,256,256]{2,1,0:T(8,128)S(1)}, f32[1,256,256]{2,1,0:T(8,128)S(1)}, u32[]{:S(2)}, u32[]{:S(2)}) collective-permute-start(f32[1,256,256]{2,1,0:T(8,128)S(1)} %collective-permute-done.7.received_ref), channel_id=1, source_target_pairs={{0,1},{1,0},{2,3},{3,2},{4,5},{5,4},{6,7},{7,6},{8,9},{9,8},{10,11... | collective-permute-start | bytes 786440 | tf_op jit(solution)/shard_map/ppermute | solution.py:475
  16.2 9.5 %collective-permute-start.6 = (f32[2,128,256]{2,1,0:T(8,128)S(1)}, f32[2,128,256]{2,1,0:T(8,128)S(1)}, u32[]{:S(2)}, u32[]{:S(2)}) collective-permute-start(f32[2,128,256]{2,1,0:T(8,128)S(1)} %collective-permute-done.5.received_ref), channel_id=1, source_target_pairs={{0,1},{1,0},{2,3},{3,2},{4,5},{5,4},{6,7},{7,6},{8,9},{9,8},{10,11... | collective-permute-start | bytes 786440 | tf_op jit(solution)/shard_map/ppermute | solution.py:475
  21.5 1.8 %collective-permute-start.3 = (f32[8,128]{1,0:T(8,128)S(1)}, f32[8,128]{1,0:T(8,128)S(1)}, u32[]{:S(2)}, u32[]{:S(2)}) collective-permute-start(f32[8,128]{1,0:T(8,128)S(1)} %get-tuple-element.22.found_ref), channel_id=1, source_target_pairs={{0,1},{1,0},{2,3},{3,2},{4,5},{5,4},{6,7},{7,6},{8,9},{9,8},{10,11... | collective-permute-start | bytes 12296 | tf_op jit(solution)/shard_map/ppermute | solution.py:475
  29.7 8.1 %collective-permute-start.9 = (f32[264,256]{1,0:T(8,128)S(1)}, f32[264,256]{1,0:T(8,128)S(1)}, u32[]{:S(2)}, u32[]{:S(2)}) collective-permute-start(f32[264,256]{1,0:T(8,128)S(1)} %get-tuple-element.37), channel_id=1, source_target_pairs={{2,0},{0,2},{6,4},{4,6},{10,8},{8,10},{14,12},{12,14},{18,16},{16,... | collective-permute-start | bytes 811016 | tf_op jit(solution)/shard_map/ppermute | solution.py:475
  37.8 4.5 %collective-permute-start.10 = (f32[264,256]{1,0:T(8,128)S(1)}, f32[264,256]{1,0:T(8,128)S(1)}, u32[]{:S(2)}, u32[]{:S(2)}) collective-permute-start(f32[264,256]{1,0:T(8,128)S(1)} %collective-permute-done.9.received_ref), channel_id=1, source_target_pairs={{0,1},{1,0},{2,3},{3,2},{4,5},{5,4},{6,7},{7,6},{8,9},{9,8},{10,11... | collective-permute-start | bytes 811016 | tf_op jit(solution)/shard_map/ppermute | solution.py:475

commit v2 on v0

--- a/solution.py
+++ b/solution.py
@@ -296,7 +296,6 @@
     grad_im = (grad_im - light_ref[...] * patch_ref[1]) * live
     send_ref[:height] = jnp.where(core == 0, grad_re[height:], grad_re[:height])
     send_ref[height : 2 * height] = jnp.where(core == 0, grad_im[height:], grad_im[:height])
-    send_ref[2 * height :] = jnp.broadcast_to(live, (8, frame))
     keep_ref[0] = grad_re[:height]
     keep_ref[1] = grad_im[:height]
 
@@ -351,7 +350,9 @@
         turned = turned_ref[index]
         begin = jnp.where(odd == 1, row, 0) if far else 0
         end = jnp.where(odd == 1, height, row) if far else height
-        places.append((start, begin, end, turned[:height] if far else turned[height:]))
+        slot = strip
+        there = ((slot >= 0) & (slot < lax.axis_size("tile") - 1)).astype(jnp.float32)
+        places.append((start, begin, end, (turned[:height] if far else turned[height:]) * there))
     chosen = []
     for slot, out_ref in ((0, first_ref), (1, second_ref)):
         direct = core == slot
@@ -403,9 +404,8 @@
         sums = [total_ref[0, :, at], total_ref[1, :, at]]
         for start, begin, end, light_ref, change_ref in windows:
             inside = (level >= begin) & (level < end)
-            live = change_ref[2 * height : 2 * height + 1, :1]
             light = covers(start, block, light_ref[:, :LANES], light_ref[:, LANES:], lane)
-            weight = weight + jnp.where(inside, light, 0.0) * live
+            weight = weight + jnp.where(inside, light, 0.0)
             for part in range(2):
                 rows = slice(part * height, (part + 1) * height)
                 change = covers(start, block, change_ref[rows, :LANES], change_ref[rows, LANES:], lane)
@@ -483,7 +483,6 @@
         received_scan = move(slot_scan, up)
         staged = move(object_tiles, swap)
         table = move(table, swap)
-        own_scan = move(slot_scan, swap)
         other_probe = move(probe_modes, swap)
         received_amplitude = move(amplitudes, onward)
         window, found = call(
@@ -491,7 +490,7 @@
             (shape(2, height, frame), shape(8, LANES)),
             [space(SMEM)] * 2 + [space(VMEM)] * 2,
             [space(VMEM)] * 2,
-        )(own_scan, received_scan, table, staged)
+        )(slot_scan, received_scan, table, staged)
         received = move(window, gather)
         swapped_found = move(found, swap)
         swapped_amplitude = move(received_amplitude, swap)
@@ -529,7 +528,7 @@
         )
         send, keep = call(
             wave_kernel,
-            (shape(2 * height + 8, frame), shape(2, height, frame)),
+            (shape(2 * height, frame), shape(2, height, frame)),
             [space(VMEM)] * 10,
             [space(VMEM)] * 2,
             [

time: 45.5 us -> 43.4 us (0.954)
  waiting for transfers between devices: 14.4 us -> 7.99 us
  starting transfers between devices: 15.7 us -> 20.1 us
  Pallas kernels: 14.1 us -> 13.3 us
  between operations: 0.8 us -> 1.46 us
    ppermute x12 -> x11, waiting for transfers between devices: 14.4 us -> 7.99 us  [move(): return lax.ppermute(value, AXES, pairs)]
    ppermute x12 -> x11, starting transfers between devices: 15.7 us -> 20.1 us  [move(): return lax.ppermute(value, AXES, pairs)]
    pallas_call x1, Pallas kernels: 1.45 us -> 0.76 us  [step(): call(select_kernel, (shape(2, height, frame), shape(8, LANES)), [space(SM...]
  transfers between devices with their start and end apart: 12 -> 11, of which waited for: 4 -> 3; matrix products, arithmetic and copies ran while one was open for 0% -> 0% of each run, Pallas kernels for 20% -> 19%
where the time goes in v2:
time: 43.4 us; the launch traced here: 43.1 us
  starting transfers between devices  20.1 us (46%)
  Pallas kernels  13.3 us (31%)
  waiting for transfers between devices  7.99 us (18%)
  between operations  1.46 us (3%)
    ppermute x11, starting transfers between devices, move(): return lax.ppermute(value, AXES, pairs)  20.1 us
    ppermute x11, waiting for transfers between devices, move(): return lax.ppermute(value, AXES, pairs)  7.99 us
    pallas_call x1, Pallas kernels, step(): call(wave_kernel, (shape(2 * height, frame), shape(2, height, frame)), [s...  3.83 us
    pallas_call x1, Pallas kernels, step(): call(base_kernel, (whole, whole, whole, shape(height, breadth), shape(hei...  2.6 us
    pallas_call x1, Pallas kernels, step(): call(fill_kernel, (whole, shape(frame, frame)), [space(VMEM)] * 2, [space...  1.45 us
    pallas_call x1, Pallas kernels, step(): call(second_kernel, (whole, whole), [space(VMEM)] * 8 + [space(pl.ANY)] *...  1.22 us
    pallas_call x1, Pallas kernels, step(): call(first_kernel, (whole, whole), [space(VMEM)] * 6 + [space(pl.ANY)] *...  1.11 us
    pallas_call x1, Pallas kernels, step(): call(strip_kernel, (strip, strip), [space(VMEM)] * 4, [space(VMEM)] * 2)  1.07 us
  transfers between devices with their start and end apart: 11, of which 3 were waited for; matrix products, arithmetic and copies ran while one was open for 0% of the time, Pallas kernels for 19%

profile of v2, /device:TPU:9, one launch (start us, length us, event | category | flops | bytes accessed | tf_op | source)
XLA Modules:
  0.0 43.1 jit_solution(9005327660632106123)
XLA Ops:
  0.7 0.7 %collective-permute-start.2 = (f32[2,128,2048]{2,1,0:T(8,128)}, f32[2,128,2048]{2,1,0:T(8,128)S(1)}, u32[]{:S(2)}, u32[]{:S(2)}) collective-permute-start(f32[2,128,2048]{2,1,0:T(8,128)} %param.7), channel_id=1, source_target_pairs={{0,1},{1,0},{2,3},{3,2},{4,5},{5,4},{6,7},{7,6},{8,9},{9,8},{10,11... | collective-permute-start | bytes 6291464 | tf_op jit(solution)/shard_map/ppermute | solution.py:475
  1.4 0.1 collective-permute-start.4
  1.5 0.4 %collective-permute-start.1 = (s32[2,8192]{1,0:T(2,128)}, s32[2,8192]{1,0:T(2,128)S(1)}, u32[]{:S(2)}, u32[]{:S(2)}) collective-permute-start(s32[2,8192]{1,0:T(2,128)} %bitcast.1), channel_id=1, source_target_pairs={{0,1},{1,0},{2,3},{3,2},{4,5},{5,4},{6,7},{7,6},{8,9},{9,8},{10,11... | collective-permute-start | bytes 196616 | tf_op jit(solution)/shard_map/ppermute | solution.py:475
  1.9 0.7 %collective-permute-start.7 = (f32[1,256,256]{2,1,0:T(8,128)}, f32[1,256,256]{2,1,0:T(8,128)S(1)}, u32[]{:S(2)}, u32[]{:S(2)}) collective-permute-start(f32[1,256,256]{2,1,0:T(8,128)} %own_ref.1), channel_id=1, source_target_pairs={{2,6},{6,10},{10,14},{14,18},{18,22},{22,26},{26,30}} | collective-permute-start | bytes 786440 | tf_op jit(solution)/shard_map/ppermute | solution.py:475
  2.6 3.1 %collective-permute-start = (s32[1]{0:T(128)}, s32[1]{0:T(128)}, u32[]{:S(2)}, u32[]{:S(2)}) collective-permute-start(s32[1]{0:T(128)} %param.11), channel_id=1, source_target_pairs={{0,2},{2,4},{4,6},{6,8},{8,10},{10,12},{12,14},{14,16},{16,18},{18... | collective-permute-start | bytes 20 | tf_op jit(solution)/shard_map/ppermute | solution.py:475
  6.4 1.5 %collective-permute-done.scan_ref = s32[1]{0:T(128)} collective-permute-done((s32[1]{0:T(128)}, s32[1]{0:T(128)}, u32[]{:S(2)}, u32[]{:S(2)}) %collective-permute-start) | collective-permute-done | bytes 36 | tf_op jit(solution)/shard_map/ppermute | solution.py:475
  7.9 0.0 collective-permute-done.1.table_ref
  7.9 0.0 collective-permute-done.2.object_ref
  7.9 0.8 %shard_map.77 = (f32[2,128,256]{2,1,0:T(8,128)S(1)}, f32[8,128]{1,0:T(8,128)S(1)}) custom-call(s32[1]{0:T(128)S(6)} %copy.18.own_scan_ref, s32[1]{0:T(128)} %collective-permute-done.scan_ref, s32[2,8192]{1,0:T(2,128)S(1)} %collective-permute-done.1.table_ref, f32[2,128,2048]{2,1,0:T(8,128)S(1)} %collective-permute-done.2.object_ref), custom_call_target="tpu_custom_call" | custom-call | flops 5000000 | bytes 5000000 | tf_op jit(solution)/shard_map/pallas_call | solution.py:488
  8.6 2.1 %collective-permute-start.5 = (f32[2,128,256]{2,1,0:T(8,128)S(1)}, f32[2,128,256]{2,1,0:T(8,128)S(1)}, u32[]{:S(2)}, u32[]{:S(2)}) collective-permute-start(f32[2,128,256]{2,1,0:T(8,128)S(1)} %get-tuple-element.27), channel_id=1, source_target_pairs={{0,2},{2,0},{4,6},{6,4},{8,10},{10,8},{12,14},{14,12},{16,18},{18,... | collective-permute-start | bytes 786440 | tf_op jit(solution)/shard_map/ppermute | solution.py:475
  10.8 0.0 collective-permute-done.7.received_ref
  10.8 4.6 %collective-permute-start.8 = (f32[1,256,256]{2,1,0:T(8,128)S(1)}, f32[1,256,256]{2,1,0:T(8,128)S(1)}, u32[]{:S(2)}, u32[]{:S(2)}) collective-permute-start(f32[1,256,256]{2,1,0:T(8,128)S(1)} %collective-permute-done.7.received_ref), channel_id=1, source_target_pairs={{0,1},{1,0},{2,3},{3,2},{4,5},{5,4},{6,7},{7,6},{8,9},{9,8},{10,11... | collective-permute-start | bytes 786440 | tf_op jit(solution)/shard_map/ppermute | solution.py:475
  15.4 0.4 collective-permute-done.5.received_ref
  15.8 5.7 %collective-permute-start.6 = (f32[2,128,256]{2,1,0:T(8,128)S(1)}, f32[2,128,256]{2,1,0:T(8,128)S(1)}, u32[]{:S(2)}, u32[]{:S(2)}) collective-permute-start(f32[2,128,256]{2,1,0:T(8,128)S(1)} %collective-permute-done.5.received_ref), channel_id=1, source_target_pairs={{0,1},{1,0},{2,3},{3,2},{4,5},{5,4},{6,7},{7,6},{8,9},{9,8},{10,11... | collective-permute-start | bytes 786440 | tf_op jit(solution)/shard_map/ppermute | solution.py:475
  21.4 0.0 collective-permute-start.3
  21.4 0.0 collective-permute-done.8.swapped_ref
  21.4 0.3 shard_map.81.amplitude_ref
  21.7 0.0 collective-permute-done.4.other_probe_ref
  21.8 1.4 %shard_map.78 = (f32[2,128,2048]{2,1,0:T(8,128)}, f32[256,256]{1,0:T(8,128)S(1)}) custom-call(f32[2,2,256,256]{3,2,1,0:T(8,128)S(1)} %copy-done, f32[2,2,256,256]{3,2,1,0:T(8,128)S(1)} %collective-permute-done.4.other_probe_ref), custom_call_target="tpu_custom_call" | custom-call | flops 5000000 | bytes 5000000 | tf_op jit(solution)/shard_map/pallas_call | solution.py:499
  23.2 0.0 collective-permute-done.3.swapped_ref
  23.2 0.0 copy-start.1
  23.2 1.0 %shard_map.79 = (f32[4,2,256,256]{3,2,1,0:T(8,128)S(1)}, f32[2,128,256]{2,1,0:T(8,128)S(1)}, f32[256,256]{1,0:T(8,128)S(1)}, f32[8,128]{1,0:T(8,128)S(1)}) custom-call(f32[8,128]{1,0:T(8,128)S(1)} %get-tuple-element.23.found_ref, f32[8,128]{1,0:T(8,128)S(1)} %collective-permute-done.3.swapped_ref, f32[2,128,2048]{2,1,0:T(8,128)S(1)} %collective-permute-done.2.object_ref, ...), custom_call_target="tpu_custom_call" | custom-call | flops 5000000 | bytes 5000000 | tf_op jit(solution)/shard_map/pallas_call | solution.py:506
  24.2 0.2 copy-done.1
  24.5 1.1 %shard_map.80 = (f32[4,2,128,256]{3,2,1,0:T(8,128)S(1)}, f32[4,2,128,256]{3,2,1,0:T(8,128)S(1)}) custom-call(f32[2,128,256]{2,1,0:T(8,128)S(1)} %get-tuple-element.26.own_ref.window_ref, f32[2,128,256]{2,1,0:T(8,128)S(1)} %collective-permute-done.5.received_ref, f32[4,2,256,256]{3,2,1,0:T(8,128)S(1)} %get-tuple-element.28.probe_ref, ...), custom_call_target="tpu_custom_call" | custom-call | flops 5000000 | bytes 5000000 | tf_op jit(solution)/shard_map/pallas_call | solution.py:526
  25.5 0.0 collective-permute-done.6.swapped_ref
  25.5 3.8 %shard_map.82 = (f32[256,256]{1,0:T(8,128)S(1)}, f32[2,128,256]{2,1,0:T(8,128)S(1)}) custom-call(f32[8,128]{1,0:T(8,128)S(1)} %get-tuple-element.25.place_ref, f32[2,128,256]{2,1,0:T(8,128)S(1)} %get-tuple-element.26.own_ref.window_ref, f32[2,128,256]{2,1,0:T(8,128)S(1)} %collective-permute-done.5.received_ref, ...), custom_call_target="tpu_custom_call" | custom-call | flops 5000000 | bytes 5000000 | tf_op jit(solution)/shard_map/pallas_call | solution.py:529
  29.4 1.9 %collective-permute-start.9 = (f32[256,256]{1,0:T(8,128)S(1)}, f32[256,256]{1,0:T(8,128)S(1)}, u32[]{:S(2)}, u32[]{:S(2)}) collective-permute-start(f32[256,256]{1,0:T(8,128)S(1)} %get-tuple-element.39), channel_id=1, source_target_pairs={{2,0},{0,2},{6,4},{4,6},{10,8},{8,10},{14,12},{12,14},{18,16},{16,... | collective-permute-start | bytes 786440 | tf_op jit(solution)/shard_map/ppermute | solution.py:475
  31.3 6.1 %collective-permute-done.9.received_ref = f32[256,256]{1,0:T(8,128)S(1)} collective-permute-done((f32[256,256]{1,0:T(8,128)S(1)}, f32[256,256]{1,0:T(8,128)S(1)}, u32[]{:S(2)}, u32[]{:S(2)}) %collective-permute-start.9) | collective-permute-done | bytes 262176 | tf_op jit(solution)/shard_map/ppermute | solution.py:475
  37.4 0.8 %collective-permute-start.10 = (f32[256,256]{1,0:T(8,128)S(1)}, f32[256,256]{1,0:T(8,128)S(1)}, u32[]{:S(2)}, u32[]{:S(2)}) collective-permute-start(f32[256,256]{1,0:T(8,128)S(1)} %collective-permute-done.9.received_ref), channel_id=1, source_target_pairs={{0,1},{1,0},{2,3},{3,2},{4,5},{5,4},{6,7},{7,6},{8,9},{9,8},{10,11... | collective-permute-start | bytes 786440 | tf_op jit(solution)/shard_map/ppermute | solution.py:475
  38.2 2.6 %shard_map.83 = (f32[2,128,2048]{2,1,0:T(8,128)}, f32[2,128,2048]{2,1,0:T(8,128)}, f32[2,128,2048]{2,1,0:T(8,128)S(1)}, f32[128,2048]{1,0:T(8,128)S(1)}, f32[128...) custom-call(f32[8,128]{1,0:T(8,128)S(1)} %get-tuple-element.25.place_ref, ...), custom_call_target="tpu_custom_call", output_to_operand_aliasing={{1}: (7, {})} | custom-call | flops 5000000 | bytes 5000000 | tf_op jit(solution)/shard_map/pallas_call | solution.py:544
  40.8 1.1 %shard_map.84 = (f32[2,128,2048]{2,1,0:T(8,128)}, f32[2,128,2048]{2,1,0:T(8,128)}) custom-call(f32[8,128]{1,0:T(8,128)S(1)} %get-tuple-element.34.others_ref, f32[2,128,2048]{2,1,0:T(8,128)S(1)} %collective-permute-done.2.object_ref, f32[2,128,2048]{2,1,0:T(8,128)S(1)} %get-tuple-element.35.total_ref, ...), custom_call_target="tpu_custom_call", output_to_operand_aliasing={{0}: (6, {}), {1}: (7, {})} | custom-call | flops 5000000 | bytes 5000000 | tf_op jit(solution)/shard_map/pallas_call | solution.py:567
  41.9 1.2 %shard_map.85 = (f32[2,128,2048]{2,1,0:T(8,128)}, f32[2,128,2048]{2,1,0:T(8,128)}) custom-call(f32[8,128]{1,0:T(8,128)S(1)} %get-tuple-element.34.others_ref, f32[2,128,2048]{2,1,0:T(8,128)S(1)} %collective-permute-done.2.object_ref, f32[2,128,2048]{2,1,0:T(8,128)S(1)} %get-tuple-element.35.total_ref, ...), custom_call_target="tpu_custom_call", output_to_operand_aliasing={{0}: (8, {}), {1}: (9, {})} | custom-call | flops 5000000 | bytes 5000000 | tf_op jit(solution)/shard_map/pallas_call | solution.py:575
  (5 shorter events, 0.0 us)
Async XLA Ops:
  0.6 21.1 %copy-start = (f32[2,2,256,256]{3,2,1,0:T(8,128)S(1)}, f32[2,2,256,256]{3,2,1,0:T(8,128)}, u32[]{:S(2)}) copy-start(f32[2,2,256,256]{3,2,1,0:T(8,128)} %own_probe_ref.3) | copy-start | bytes 3145732
  0.6 20.8 %copy-start.2 = (f32[1,256,256]{2,1,0:T(8,128)S(1)}, f32[1,256,256]{2,1,0:T(8,128)}, u32[]{:S(2)}) copy-start(f32[1,256,256]{2,1,0:T(8,128)} %own_ref.1) | copy-start | bytes 786436
  0.7 7.2 %collective-permute-start.2 = (f32[2,128,2048]{2,1,0:T(8,128)}, f32[2,128,2048]{2,1,0:T(8,128)S(1)}, u32[]{:S(2)}, u32[]{:S(2)}) collective-permute-start(f32[2,128,2048]{2,1,0:T(8,128)} %param.7), channel_id=1, source_target_pairs={{0,1},{1,0},{2,3},{3,2},{4,5},{5,4},{6,7},{7,6},{8,9},{9,8},{10,11... | collective-permute-start | bytes 6291464 | tf_op jit(solution)/shard_map/ppermute | solution.py:475
  1.4 20.4 %collective-permute-start.4 = (f32[2,2,256,256]{3,2,1,0:T(8,128)}, f32[2,2,256,256]{3,2,1,0:T(8,128)S(1)}, u32[]{:S(2)}, u32[]{:S(2)}) collective-permute-start(f32[2,2,256,256]{3,2,1,0:T(8,128)} %own_probe_ref.3), channel_id=1, source_target_pairs={{0,1},{1,0},{2,3},{3,2},{4,5},{5,4},{6,7},{7,6},{8,9},{9,8},{10,11... | collective-permute-start | bytes 3145736 | tf_op jit(solution)/shard_map/ppermute | solution.py:475
  1.5 6.4 %collective-permute-start.1 = (s32[2,8192]{1,0:T(2,128)}, s32[2,8192]{1,0:T(2,128)S(1)}, u32[]{:S(2)}, u32[]{:S(2)}) collective-permute-start(s32[2,8192]{1,0:T(2,128)} %bitcast.1), channel_id=1, source_target_pairs={{0,1},{1,0},{2,3},{3,2},{4,5},{5,4},{6,7},{7,6},{8,9},{9,8},{10,11... | collective-permute-start | bytes 196616 | tf_op jit(solution)/shard_map/ppermute | solution.py:475
  1.9 8.9 %collective-permute-start.7 = (f32[1,256,256]{2,1,0:T(8,128)}, f32[1,256,256]{2,1,0:T(8,128)S(1)}, u32[]{:S(2)}, u32[]{:S(2)}) collective-permute-start(f32[1,256,256]{2,1,0:T(8,128)} %own_ref.1), channel_id=1, source_target_pairs={{2,6},{6,10},{10,14},{14,18},{18,22},{22,26},{26,30}} | collective-permute-start | bytes 786440 | tf_op jit(solution)/shard_map/ppermute | solution.py:475
  2.6 5.3 %collective-permute-start = (s32[1]{0:T(128)}, s32[1]{0:T(128)}, u32[]{:S(2)}, u32[]{:S(2)}) collective-permute-start(s32[1]{0:T(128)} %param.11), channel_id=1, source_target_pairs={{0,2},{2,4},{4,6},{6,8},{8,10},{10,12},{12,14},{14,16},{16,18},{18... | collective-permute-start | bytes 20 | tf_op jit(solution)/shard_map/ppermute | solution.py:475
  8.6 7.1 %collective-permute-start.5 = (f32[2,128,256]{2,1,0:T(8,128)S(1)}, f32[2,128,256]{2,1,0:T(8,128)S(1)}, u32[]{:S(2)}, u32[]{:S(2)}) collective-permute-start(f32[2,128,256]{2,1,0:T(8,128)S(1)} %get-tuple-element.27), channel_id=1, source_target_pairs={{0,2},{2,0},{4,6},{6,4},{8,10},{10,8},{12,14},{14,12},{16,18},{18,... | collective-permute-start | bytes 786440 | tf_op jit(solution)/shard_map/ppermute | solution.py:475
  10.8 10.6 %collective-permute-start.8 = (f32[1,256,256]{2,1,0:T(8,128)S(1)}, f32[1,256,256]{2,1,0:T(8,128)S(1)}, u32[]{:S(2)}, u32[]{:S(2)}) collective-permute-start(f32[1,256,256]{2,1,0:T(8,128)S(1)} %collective-permute-done.7.received_ref), channel_id=1, source_target_pairs={{0,1},{1,0},{2,3},{3,2},{4,5},{5,4},{6,7},{7,6},{8,9},{9,8},{10,11... | collective-permute-start | bytes 786440 | tf_op jit(solution)/shard_map/ppermute | solution.py:475
  15.8 9.8 %collective-permute-start.6 = (f32[2,128,256]{2,1,0:T(8,128)S(1)}, f32[2,128,256]{2,1,0:T(8,128)S(1)}, u32[]{:S(2)}, u32[]{:S(2)}) collective-permute-start(f32[2,128,256]{2,1,0:T(8,128)S(1)} %collective-permute-done.5.received_ref), channel_id=1, source_target_pairs={{0,1},{1,0},{2,3},{3,2},{4,5},{5,4},{6,7},{7,6},{8,9},{9,8},{10,11... | collective-permute-start | bytes 786440 | tf_op jit(solution)/shard_map/ppermute | solution.py:475
  21.4 1.8 %collective-permute-start.3 = (f32[8,128]{1,0:T(8,128)S(1)}, f32[8,128]{1,0:T(8,128)S(1)}, u32[]{:S(2)}, u32[]{:S(2)}) collective-permute-start(f32[8,128]{1,0:T(8,128)S(1)} %get-tuple-element.23.found_ref), channel_id=1, source_target_pairs={{0,1},{1,0},{2,3},{3,2},{4,5},{5,4},{6,7},{7,6},{8,9},{9,8},{10,11... | collective-permute-start | bytes 12296 | tf_op jit(solution)/shard_map/ppermute | solution.py:475
  23.2 1.2 %copy-start.1 = (bf16[8,256,256]{2,1,0:T(8,128)(2,1)S(1)}, bf16[8,256,256]{2,1,0:T(8,128)(2,1)}, u32[]{:S(2)}) copy-start(bf16[8,256,256]{2,1,0:T(8,128)(2,1)} %constant.2.clone.matrix_ref) | copy-start | bytes 3145732
  29.4 8.0 %collective-permute-start.9 = (f32[256,256]{1,0:T(8,128)S(1)}, f32[256,256]{1,0:T(8,128)S(1)}, u32[]{:S(2)}, u32[]{:S(2)}) collective-permute-start(f32[256,256]{1,0:T(8,128)S(1)} %get-tuple-element.39), channel_id=1, source_target_pairs={{2,0},{0,2},{6,4},{4,6},{10,8},{8,10},{14,12},{12,14},{18,16},{16,... | collective-permute-start | bytes 786440 | tf_op jit(solution)/shard_map/ppermute | solution.py:475
  37.4 4.5 %collective-permute-start.10 = (f32[256,256]{1,0:T(8,128)S(1)}, f32[256,256]{1,0:T(8,128)S(1)}, u32[]{:S(2)}, u32[]{:S(2)}) collective-permute-start(f32[256,256]{1,0:T(8,128)S(1)} %collective-permute-done.9.received_ref), channel_id=1, source_target_pairs={{0,1},{1,0},{2,3},{3,2},{4,5},{5,4},{6,7},{7,6},{8,9},{9,8},{10,11... | collective-permute-start | bytes 786440 | tf_op jit(solution)/shard_map/ppermute | solution.py:475
